TPU v7x, 32 devices: a whole 2x2x4 slice. The times are simulated.
32 devices in a mesh: seq: 2 (over y), shard: 16 (over z, x, core).
Axes of the slice: x: 2, y: 2, z: 4, core: 2. Of those that a mesh axis runs over, the one named last changes fastest.
Arguments:
- tokens: bfloat16 [32768, 768], P(('seq', 'shard')), may hold values from -6 to 6
- qkv_weight: bfloat16 [2, 768, 2304], P(None, 'shard'), may hold values from -0.21875 to 0.21875
- out_weight: bfloat16 [2, 768, 768], P(None, 'shard'), may hold values from -0.875 to 0.875
- up_weight: bfloat16 [2, 768, 3072], P(None, 'shard'), may hold values from -0.21875 to 0.21875
- down_weight: bfloat16 [2, 3072, 768], P(None, 'shard'), may hold values from -0.109375 to 0.109375
- norm_gains: bfloat16 [2, 2, 768], P(None, None, 'shard'), may hold values from 0.5 to 1.5
- biases: bfloat16 [2, 5, 768], P(None, None, 'shard'), may hold values from -2.5 to 2.5
- up_bias: bfloat16 [2, 3072], P(None, 'shard'), may hold values from -2.5 to 2.5
- position_table: bfloat16 [64, 768], P(None, 'shard'), may hold values from -4 to 4
- segment_docs: int32 [2, 128], P('seq'), may hold values from 0 to 7, never falling along the last dimension, each value on 1 to 64 neighbouring positions
- cotangent: bfloat16 [32768, 768], P(('seq', 'shard')), may hold values from -6 to 6
Outputs:
- merged: bfloat16 [32768, 768], P(('seq', 'shard'))
- grad_tokens: bfloat16 [32768, 768], P(('seq', 'shard'))
- grad_qkv: float32 [2, 768, 2304], P(None, 'shard')
- grad_out: float32 [2, 768, 768], P(None, 'shard')
- grad_up: float32 [2, 768, 3072], P(None, 'shard')
- grad_down: float32 [2, 3072, 768], P(None, 'shard')
- grad_gains: float32 [2, 2, 768], P(None, None, 'shard')
- grad_biases: float32 [2, 5, 768], P(None, None, 'shard')
- grad_up_bias: float32 [2, 3072], P(None, 'shard')
- grad_table: float32 [64, 768], P(None, 'shard')
Inputs may be any that keep to these rules, and one draw needn't show every extreme that they name: `segment_docs`: along each sequence the document numbers never fall, each document covers 1 to 64 segments, and one covers exactly 64.
All inputs are finite; a program needn't handle non-finite values.
Results may differ from a plain program's by a relative error of at most 0.024.
Values may be sent and summed in bfloat16 or wider, within the bound.
No kernel may reach another device: no remote copies, remote signals or barrier semaphores. Data moves between devices by JAX's collectives and lax.ppermute only.
A program may use at most 256 MiB of HBM per device.

v0:
```python
from functools import partial

import jax
import jax.numpy as jnp
from jax import lax
from jax.sharding import PartitionSpec as P

HEAD = 64
SEG = 128


EPSILON = 1e-05
MASKED = -1e30
HIGHEST = lax.Precision.HIGHEST


def contract_rows(left_side, right_side):
    return lax.dot_general(
        left_side, right_side, (((0,), (0,)), ((), ())), preferred_element_type=jnp.float32
    )


def times_transposed(left_side, right_side):
    return lax.dot_general(
        left_side, right_side, (((1,), (1,)), ((), ())), preferred_element_type=jnp.float32
    )


def column_sums(matrix):
    return jnp.sum(matrix.astype(jnp.float32), axis=0)


def norm_rows(summed, norm_gain, norm_shift):
    centred = summed - jnp.mean(summed, axis=-1, keepdims=True)
    spread = jnp.mean(centred * centred, axis=-1, keepdims=True)
    inverse = lax.rsqrt(spread + EPSILON)
    normed = centred * inverse
    return (normed * norm_gain + norm_shift, normed, inverse)


def norm_back(incoming, normed, inverse, norm_gain):
    scaled = incoming * norm_gain
    mean_part = jnp.mean(scaled, axis=-1, keepdims=True)
    slope_part = jnp.mean(scaled * normed, axis=-1, keepdims=True)
    d_summed = inverse * (scaled - mean_part - normed * slope_part)
    return (d_summed, jnp.sum(incoming * normed, axis=0), jnp.sum(incoming, axis=0))


def raw_scores(queries, key_rows, allowed):
    factor = queries.shape[-1] ** (-0.5)
    scores = (
        jnp.einsum("brhe,bkhe->bhrk", queries, key_rows, preferred_element_type=jnp.float32)
        * factor
    )
    if allowed is None:
        return scores
    return jnp.where(allowed, scores, MASKED)


def attend_forward(queries, key_rows, value_rows, allowed):
    scores = raw_scores(queries, key_rows, allowed)
    highest = jnp.max(scores, axis=-1, keepdims=True)
    log_total = highest + jnp.log(jnp.sum(jnp.exp(scores - highest), axis=-1, keepdims=True))
    weights = jnp.exp(scores - log_total).astype(jnp.bfloat16)
    attended = jnp.einsum(
        "bhrk,bkhe->brhe", weights, value_rows, preferred_element_type=jnp.float32
    )
    return (attended, log_total)


def attend_backward(queries, key_rows, value_rows, log_total, d_attended, allowed):
    factor = queries.shape[-1] ** (-0.5)
    weights = jnp.exp(raw_scores(queries, key_rows, allowed) - log_total)
    d_weights = jnp.einsum(
        "brhe,bkhe->bhrk", d_attended, value_rows, preferred_element_type=jnp.float32
    )
    row_inner = jnp.sum(weights * d_weights, axis=-1, keepdims=True)
    d_scores = (weights * (d_weights - row_inner)).astype(jnp.bfloat16)
    d_queries = (
        jnp.einsum("bhrk,bkhe->brhe", d_scores, key_rows, preferred_element_type=jnp.float32)
        * factor
    )
    d_keys = (
        jnp.einsum("bhrk,brhe->bkhe", d_scores, queries, preferred_element_type=jnp.float32)
        * factor
    )
    d_values = jnp.einsum(
        "bhrk,brhe->bkhe",
        weights.astype(jnp.bfloat16),
        d_attended,
        preferred_element_type=jnp.float32,
    )
    return (d_queries, d_keys, d_values)


def segment_mix(queries, key_rows, value_rows):
    stacked = jnp.stack([queries, key_rows, value_rows])
    stacked = lax.all_to_all(stacked, "seq", split_axis=2, concat_axis=1, tiled=True)
    row_count = stacked.shape[1]
    col_count = stacked.shape[2]
    grouped = stacked.reshape(3, row_count // SEG, SEG, col_count // HEAD, HEAD)
    attended, log_total = attend_forward(grouped[0], grouped[1], grouped[2], None)
    attended = attended.reshape(row_count, col_count).astype(jnp.bfloat16)
    attended = lax.all_to_all(attended, "seq", split_axis=0, concat_axis=1, tiled=True)
    return (attended, (grouped, log_total))


def segment_back(d_attended, kept_state):
    grouped, log_total = kept_state
    d_attended = lax.all_to_all(d_attended, "seq", split_axis=1, concat_axis=0, tiled=True)
    row_count = d_attended.shape[0]
    col_count = d_attended.shape[1]
    d_grouped = d_attended.reshape(row_count // SEG, SEG, col_count // HEAD, HEAD)
    d_queries, d_keys, d_values = attend_backward(
        grouped[0], grouped[1], grouped[2], log_total, d_grouped, None
    )
    stacked = (
        jnp.stack([d_queries, d_keys, d_values])
        .astype(jnp.bfloat16)
        .reshape(3, row_count, col_count)
    )
    stacked = lax.all_to_all(stacked, "seq", split_axis=1, concat_axis=2, tiled=True)
    return (stacked[0], stacked[1], stacked[2])


def cross_mix(queries, key_rows, value_rows, allowed):
    row_count = queries.shape[0]
    col_count = queries.shape[1]
    view_shape = (1, row_count, col_count // HEAD, HEAD)
    grouped = (
        queries.reshape(view_shape),
        key_rows.reshape(view_shape),
        value_rows.reshape(view_shape),
    )
    attended, log_total = attend_forward(grouped[0], grouped[1], grouped[2], allowed)
    return (attended.reshape(row_count, col_count).astype(jnp.bfloat16), (grouped, log_total))


def cross_back(d_attended, kept_state, allowed):
    grouped, log_total = kept_state
    row_count = d_attended.shape[0]
    col_count = d_attended.shape[1]
    d_grouped = d_attended.reshape(1, row_count, col_count // HEAD, HEAD)
    d_queries, d_keys, d_values = attend_backward(
        grouped[0], grouped[1], grouped[2], log_total, d_grouped, allowed
    )
    return (
        d_queries.reshape(row_count, col_count).astype(jnp.bfloat16),
        d_keys.reshape(row_count, col_count).astype(jnp.bfloat16),
        d_values.reshape(row_count, col_count).astype(jnp.bfloat16),
    )


def block_forward(entry_rows, inputs, weights, mix_step):
    qkv_full = weights[0]
    out_full = weights[1]
    up_full = weights[2]
    down_full = weights[3]
    gain_rows = weights[4].astype(jnp.float32)
    bias_rows = weights[5].astype(jnp.float32)
    model_width = entry_rows.shape[1]
    projected = jnp.dot(entry_rows, qkv_full, preferred_element_type=jnp.float32)
    queries = projected[:, :model_width].astype(jnp.bfloat16)
    key_rows = projected[:, model_width : 2 * model_width].astype(jnp.bfloat16)
    value_rows = (projected[:, 2 * model_width :] + bias_rows[0]).astype(jnp.bfloat16)
    attended, kept_state = mix_step(queries, key_rows, value_rows)
    branch = jnp.dot(attended, out_full, preferred_element_type=jnp.float32) + bias_rows[1]
    first_out, first_normed, first_inverse = norm_rows(inputs + branch, gain_rows[0], bias_rows[3])
    first_low = first_out.astype(jnp.bfloat16)
    hidden = jnp.dot(first_low, up_full, preferred_element_type=jnp.float32) + weights[6].astype(
        jnp.float32
    )
    active = jax.nn.gelu(hidden, approximate=False).astype(jnp.bfloat16)
    feed_out = jnp.dot(active, down_full, preferred_element_type=jnp.float32) + bias_rows[2]
    final_out, second_normed, second_inverse = norm_rows(
        first_out + feed_out, gain_rows[1], bias_rows[4]
    )
    kept_values = (
        entry_rows,
        attended,
        kept_state,
        first_normed,
        first_inverse,
        first_low,
        hidden,
        active,
        second_normed,
        second_inverse,
    )
    return (final_out, kept_values)


def block_backward(incoming, kept_values, weights, mix_back):
    qkv_full = weights[0]
    out_full = weights[1]
    up_full = weights[2]
    down_full = weights[3]
    gain_rows = weights[4].astype(jnp.float32)
    (
        entry_rows,
        attended,
        kept_state,
        first_normed,
        first_inverse,
        first_low,
        hidden,
        active,
        second_normed,
        second_inverse,
    ) = kept_values
    d_second, d_gain_two, d_shift_two = norm_back(
        incoming, second_normed, second_inverse, gain_rows[1]
    )
    d_feed = d_second.astype(jnp.bfloat16)
    grad_down = contract_rows(active, d_feed)
    d_active = times_transposed(d_feed, down_full)
    gelu_pull = jax.vjp(partial(jax.nn.gelu, approximate=False), hidden)[1]
    d_hidden = gelu_pull(d_active)[0].astype(jnp.bfloat16)
    grad_up = contract_rows(first_low, d_hidden)
    d_first = d_second + times_transposed(d_hidden, up_full)
    d_sum_one, d_gain_one, d_shift_one = norm_back(
        d_first, first_normed, first_inverse, gain_rows[0]
    )
    d_branch = d_sum_one.astype(jnp.bfloat16)
    grad_out = contract_rows(attended, d_branch)
    d_attended = times_transposed(d_branch, out_full).astype(jnp.bfloat16)
    d_queries, d_keys, d_values = mix_back(d_attended, kept_state)
    d_projected = jnp.concatenate([d_queries, d_keys, d_values], axis=1)
    grad_qkv = contract_rows(entry_rows, d_projected)
    d_inputs = d_sum_one + times_transposed(d_projected, qkv_full)
    grad_gains = jnp.stack([d_gain_one, d_gain_two])
    grad_biases = jnp.stack(
        [
            column_sums(d_values),
            column_sums(d_branch),
            column_sums(d_feed),
            d_shift_one,
            d_shift_two,
        ]
    )
    return (
        d_inputs,
        (grad_qkv, grad_out, grad_up, grad_down, grad_gains, grad_biases, column_sums(d_hidden)),
    )


def own_piece(gradient, axis_dim, shard_index, group_count):
    length = gradient.shape[axis_dim] // group_count
    return lax.dynamic_slice_in_dim(gradient, shard_index * length, length, axis_dim)


def body(
    tokens,
    qkv_weight,
    out_weight,
    up_weight,
    down_weight,
    norm_gains,
    biases,
    up_bias,
    position_table,
    segment_docs,
    cotangent,
):
    seg_weights = (
        lax.all_gather(qkv_weight[0], "shard", axis=0, tiled=True),
        lax.all_gather(out_weight[0], "shard", axis=0, tiled=True),
        lax.all_gather(up_weight[0], "shard", axis=0, tiled=True),
        lax.all_gather(down_weight[0], "shard", axis=0, tiled=True),
        lax.all_gather(norm_gains[0], "shard", axis=1, tiled=True),
        lax.all_gather(biases[0], "shard", axis=1, tiled=True),
        lax.all_gather(up_bias[0], "shard", axis=0, tiled=True),
    )
    inputs = tokens.astype(jnp.float32)
    seg_out, seg_kept = block_forward(tokens, inputs, seg_weights, segment_mix)
    local_segs = tokens.shape[0] // SEG
    model_width = tokens.shape[1]
    seg_grid = seg_out.reshape(local_segs, SEG, model_width)
    heads_local = seg_grid[:, 0, :].astype(jnp.bfloat16)
    grad_local = cotangent.reshape(local_segs, SEG, model_width)[:, 0, :]
    heads_all, grad_heads = (
        lax.all_gather(heads_local, "shard", axis=0, tiled=True),
        lax.all_gather(grad_local, "shard", axis=0, tiled=True),
    )
    cross_all = (
        lax.all_gather(qkv_weight[1], "shard", axis=0, tiled=True),
        lax.all_gather(out_weight[1], "shard", axis=0, tiled=True),
        lax.all_gather(up_weight[1], "shard", axis=0, tiled=True),
        lax.all_gather(down_weight[1], "shard", axis=0, tiled=True),
        lax.all_gather(norm_gains[1], "shard", axis=1, tiled=True),
        lax.all_gather(biases[1], "shard", axis=1, tiled=True),
        lax.all_gather(up_bias[1], "shard", axis=0, tiled=True),
        lax.all_gather(position_table, "shard", axis=1, tiled=True),
    )
    cross_weights = cross_all[:7]
    full_table = cross_all[7]
    doc_ids = segment_docs[0]
    seg_count = doc_ids.shape[0]
    same_doc = doc_ids[:, None] == doc_ids[None, :]
    ordinal = lax.iota(jnp.int32, seg_count)
    position = jnp.sum((same_doc & (ordinal[:, None] > ordinal[None, :])).astype(jnp.int32), axis=1)
    lookup = position[:, None] == lax.iota(jnp.int32, full_table.shape[0])[None, :]
    places = jnp.dot(lookup.astype(jnp.bfloat16), full_table, preferred_element_type=jnp.float32)
    cross_in = heads_all.astype(jnp.float32) + places
    allowed = same_doc[None, None]
    cross_out, cross_kept = block_forward(
        cross_in.astype(jnp.bfloat16), cross_in, cross_weights, partial(cross_mix, allowed=allowed)
    )
    shard_index = lax.axis_index("shard")
    start_row = shard_index * local_segs
    own_rows = lax.dynamic_slice_in_dim(cross_out, start_row, local_segs, 0)
    merged = seg_grid.at[:, 0, :].set(own_rows).reshape(-1, model_width).astype(jnp.bfloat16)
    d_cross_in, cross_grads = block_backward(
        grad_heads.astype(jnp.float32),
        cross_kept,
        cross_weights,
        partial(cross_back, allowed=allowed),
    )
    grad_table = lax.dot_general(
        lookup.astype(jnp.float32),
        d_cross_in,
        (((0,), (0,)), ((), ())),
        precision=HIGHEST,
        preferred_element_type=jnp.float32,
    )
    d_own_rows = lax.dynamic_slice_in_dim(d_cross_in, start_row, local_segs, 0)
    d_seg_out = (
        cotangent.astype(jnp.float32)
        .reshape(local_segs, SEG, model_width)
        .at[:, 0, :]
        .set(d_own_rows)
        .reshape(-1, model_width)
    )
    d_tokens, seg_grads = block_backward(d_seg_out, seg_kept, seg_weights, segment_back)
    shard_count = lax.axis_size("shard")
    cross_dims = (0, 0, 0, 0, 1, 1, 0, 1)
    cross_terms = [
        own_piece(gradient, axis_dim, shard_index, shard_count)
        for gradient, axis_dim in zip(cross_grads + (grad_table,), cross_dims)
    ]
    cross_sum = (
        lax.psum(cross_terms[0].astype(jnp.bfloat16), "seq").astype(jnp.float32),
        lax.psum(cross_terms[1].astype(jnp.bfloat16), "seq").astype(jnp.float32),
        lax.psum(cross_terms[2].astype(jnp.bfloat16), "seq").astype(jnp.float32),
        lax.psum(cross_terms[3].astype(jnp.bfloat16), "seq").astype(jnp.float32),
        lax.psum(cross_terms[4].astype(jnp.bfloat16), "seq").astype(jnp.float32),
        lax.psum(cross_terms[5].astype(jnp.bfloat16), "seq").astype(jnp.float32),
        lax.psum(cross_terms[6].astype(jnp.bfloat16), "seq").astype(jnp.float32),
        lax.psum(cross_terms[7].astype(jnp.bfloat16), "seq").astype(jnp.float32),
    )
    pieces = (
        lax.psum_scatter(seg_grads[0], "shard", scatter_dimension=0, tiled=True),
        lax.psum_scatter(seg_grads[1], "shard", scatter_dimension=0, tiled=True),
        lax.psum_scatter(seg_grads[2], "shard", scatter_dimension=0, tiled=True),
        lax.psum_scatter(seg_grads[3], "shard", scatter_dimension=0, tiled=True),
        lax.psum_scatter(seg_grads[4], "shard", scatter_dimension=1, tiled=True),
        lax.psum_scatter(seg_grads[5], "shard", scatter_dimension=1, tiled=True),
        lax.psum_scatter(seg_grads[6], "shard", scatter_dimension=0, tiled=True),
    )
    seg_sum = (
        lax.psum(pieces[0].astype(jnp.bfloat16), "seq").astype(jnp.float32),
        lax.psum(pieces[1].astype(jnp.bfloat16), "seq").astype(jnp.float32),
        lax.psum(pieces[2].astype(jnp.bfloat16), "seq").astype(jnp.float32),
        lax.psum(pieces[3].astype(jnp.bfloat16), "seq").astype(jnp.float32),
        lax.psum(pieces[4].astype(jnp.bfloat16), "seq").astype(jnp.float32),
        lax.psum(pieces[5].astype(jnp.bfloat16), "seq").astype(jnp.float32),
        lax.psum(pieces[6].astype(jnp.bfloat16), "seq").astype(jnp.float32),
    )
    return (
        merged,
        d_tokens.astype(jnp.bfloat16),
        jnp.stack([seg_sum[0], cross_sum[0]]),
        jnp.stack([seg_sum[1], cross_sum[1]]),
        jnp.stack([seg_sum[2], cross_sum[2]]),
        jnp.stack([seg_sum[3], cross_sum[3]]),
        jnp.stack([seg_sum[4], cross_sum[4]]),
        jnp.stack([seg_sum[5], cross_sum[5]]),
        jnp.stack([seg_sum[6], cross_sum[6]]),
        cross_sum[7],
    )


def solution(mesh):
    in_specs = (
        P(("seq", "shard"), None),
        P(None, "shard", None),
        P(None, "shard", None),
        P(None, "shard", None),
        P(None, "shard", None),
        P(None, None, "shard"),
        P(None, None, "shard"),
        P(None, "shard"),
        P(None, "shard"),
        P("seq", None),
        P(("seq", "shard"), None),
    )
    out_specs = (
        P(("seq", "shard"), None),
        P(("seq", "shard"), None),
        P(None, "shard", None),
        P(None, "shard", None),
        P(None, "shard", None),
        P(None, "shard", None),
        P(None, None, "shard"),
        P(None, None, "shard"),
        P(None, "shard"),
        P(None, "shard"),
    )
    return jax.shard_map(body, mesh=mesh, in_specs=in_specs, out_specs=out_specs, check_vma=False)
```

profile of v0, /device:TPU:0, one launch (start us, length us, event | category | flops | bytes accessed | tf_op | source)
XLA Modules:
  0.0 1181.6 jit_solution(4778397032044747556)
XLA Ops:
  15.9 24.8 %all-gather.1 = bf16[1,5,768]{1,0,2:T(2,128)(2,1)S(1)} all-gather(bf16[1,5,48]{1,0,2:T(2,128)(2,1)S(1)} %copy.166), channel_id=3, replica_groups=mesh['seq'=2,'shard'=16] {'shard'}, dimensions={2}, use_global_device_ids=true | all-gather | bytes 8160 | tf_op jit(solution)/shard_map/all_gather | solution.py:271
  41.1 11.9 %slice_reduce_fusion.7 = (f32[768]{0:T(1024)S(1)}, f32[768]{0:T(1024)S(1)}, f32[768]{0:T(1024)S(1)}, f32[768]{0:T(1024)S(1)}, f32[768]{0:T(1024)S(1)}) fusion(f32[1,5,768]{1,0,2:T(1,128)S(1)} %convert_element_type.342), kind=kLoop, calls=%fused_computation.173 | loop fusion | bytes 30720 | tf_op jit(solution)/shard_map/slice | solution.py:176
  70.2 11.2 copy.112
  90.7 20.8 %all-gather.3 = bf16[1,2,768]{1,0,2:T(2,128)(2,1)S(1)} all-gather(bf16[1,2,48]{1,0,2:T(2,128)(2,1)S(1)} %copy.167), channel_id=5, replica_groups=mesh['seq'=2,'shard'=16] {'shard'}, dimensions={2}, use_global_device_ids=true | all-gather | bytes 3264 | tf_op jit(solution)/shard_map/all_gather | solution.py:270
  113.8 19.9 %all-gather.15 = bf16[128,1,768]{2,0,1:T(8,128)(2,1)} all-gather(bf16[8,1,768]{2,0,1:T(8,128)(2,1)S(1)} %copy.170), channel_id=17, replica_groups=mesh['seq'=2,'shard'=16] {'shard'}, dimensions={0}, use_global_device_ids=true | all-gather | bytes 208896 | tf_op jit(solution)/shard_map/all_gather | solution.py:283
  138.4 19.9 %all-to-all-done = bf16[3,1024,768]{1,0,2:T(4,128)(2,1)} async-done(((bf16[3,1024,768]{1,0,2:T(4,128)(2,1)}), bf16[3,1024,768]{1,0,2:T(4,128)(2,1)}, u32[]{:S(2)}, u32[]{:S(2)}) %all-to-all-start) | async-done | bytes 4718624 | tf_op jit(solution)/shard_map/all_to_all | solution.py:98
  197.2 60.4 %all-reduce.3 = (bf16[3072]{0:T(1024)(128)(2,1)S(1)}, bf16[3072]{0:T(1024)(128)(2,1)S(1)}) all-reduce(bf16[3072]{0:T(1024)(128)(2,1)S(1)} %dynamic-update-slice.6, bf16[3072]{0:T(1024)(128)(2,1)S(1)} %dynamic-update-slice.7), channel_id=7, replica_groups=mesh['seq'=2,'shard'=16] {'shard'}, use_global_device_ids=true, to_apply=%add | all-reduce | flops 6144 | bytes 24576
  257.7 18.7 %all-gather.9 = bf16[1,5,768]{1,0,2:T(2,128)(2,1)S(1)} all-gather(bf16[1,5,48]{1,0,2:T(2,128)(2,1)S(1)} %copy.168), channel_id=11, replica_groups=mesh['seq'=2,'shard'=16] {'shard'}, dimensions={2}, use_global_device_ids=true | all-gather | bytes 8160 | tf_op jit(solution)/shard_map/all_gather | solution.py:291
  277.5 20.3 %all-gather.11 = bf16[1,2,768]{1,0,2:T(2,128)(2,1)S(1)} all-gather(bf16[1,2,48]{1,0,2:T(2,128)(2,1)S(1)} %copy.169), channel_id=13, replica_groups=mesh['seq'=2,'shard'=16] {'shard'}, dimensions={2}, use_global_device_ids=true | all-gather | bytes 3264 | tf_op jit(solution)/shard_map/all_gather | solution.py:290
  298.2 18.6 %all_gather.59 = bf16[64,768]{0,1:T(8,128)(2,1)S(1)} all-gather(bf16[64,48]{0,1:T(8,128)(2,1)S(1)} %copy-done.91), channel_id=1, replica_groups=mesh['seq'=2,'shard'=16] {'shard'}, dimensions={1}, use_global_device_ids=true | all-gather | bytes 104448 | tf_op jit(solution)/shard_map/all_gather | solution.py:293
  321.5 12.4 %slice_reduce_fusion = (f32[768]{0:T(1024)}, f32[768]{0:T(1024)}, f32[768]{0:T(1024)S(1)}, f32[768]{0:T(1024)}, f32[768]{0:T(1024)S(1)}) fusion(f32[1,5,768]{1,0,2:T(1,128)S(1)} %convert_element_type.346), kind=kLoop, calls=%fused_computation.164 | loop fusion | bytes 30720 | tf_op jit(solution)/shard_map/slice | solution.py:176
  339.5 36.3 %multiply_convert_fusion = (bf16[1024,3072]{1,0:T(8,128)(2,1)}, f32[1024,3072]{1,0:T(8,128)}, f32[1024,3072]{1,0:T(8,128)}) fusion(f32[3072]{0:T(1024)S(1)} %convert_element_type.350, bf16[1,768,3072]{2,1,0:T(8,128)(2,1)} %all-gather.29.cloned.1.call-done, f32[1024,768]{1,0:T(8,128)S(1)} %get-tuple-element.164, f32[768]{0:T(1024)S(1)} %get-tuple-element.99, ...), kind=kOutput, calls=%fused_computation.4 | convolution fusion | flops 5043388416 | bytes 39348224 | tf_op jit(solution)/shard_map/dot_general | solution.py:170
  387.9 19.4 %all-gather.7 = bf16[128,1,768]{2,0,1:T(8,128)(2,1)S(1)} all-gather(bf16[8,1,768]{2,0,1:T(8,128)(2,1)S(1)} %copy.191), channel_id=9, replica_groups=mesh['seq'=2,'shard'=16] {'shard'}, dimensions={0}, use_global_device_ids=true | all-gather | bytes 208896 | tf_op jit(solution)/shard_map/all_gather | solution.py:282
  452.4 17.7 %convert_reduce_fusion = (f32[3072]{0:T(1024)}, bf16[1024,3072]{1,0:T(8,128)(2,1)}) fusion(f32[1024,3072]{1,0:T(8,128)} %get-tuple-element.134, bf16[1,3072,768]{2,1,0:T(8,128)(2,1)} %all-gather.31.cloned.1.call-done, f32[1024,768]{1,0:T(8,128)} %get-tuple-element.123, f32[1024,3072]{1,0:T(8,128)} %get-tuple-element.165, f32[3072]{0:T(1024)} %copy-done.94), kind=kOutput, calls=%fused_computation.2 | convolution fusion | flops 4886098944 | bytes 39346176 | tf_op jit(solution)/shard_map/dot_general | solution.py:24
  493.7 15.2 %all-to-all-done.2 = bf16[1024,2,384]{0,2,1:T(8,128)(2,1)S(1)} async-done(((bf16[1024,2,384]{0,2,1:T(8,128)(2,1)}), bf16[1024,2,384]{0,2,1:T(8,128)(2,1)S(1)}, u32[]{:S(2)}, u32[]{:S(2)}) %all-to-all-start.2) | async-done | bytes 1572896 | tf_op jit(solution)/shard_map/all_to_all | solution.py:110
  563.1 74.2 %all_to_all.62 = bf16[3,2048,384]{2,0,1:T(4,128)(2,1)S(1)} all-to-all(bf16[3,2048,384]{2,0,1:T(4,128)(2,1)} %copy.145), channel_id=1, replica_groups=mesh['seq'=2,'shard'=16] {'seq'}, dimensions={1} | all-to-all | bytes 9437184 | tf_op jit(solution)/shard_map/all_to_all | solution.py:122
  665.5 11.0 fusion.143
  678.7 10.9 fusion.129
  693.6 59.7 %all-reduce.2 = bf16[3072]{0:T(1024)(128)(2,1)S(1)} all-reduce(f32[3072]{0:T(1024)S(1)} %copy-done.95), channel_id=24, replica_groups=mesh['seq'=2,'shard'=16] {'shard'}, use_global_device_ids=true, to_apply=%region_56.57.clone | all-reduce | flops 3072 | bytes 18432
  773.1 93.1 %reduce-scatter.15.cloned.1.call-done = f32[48,3072]{1,0:T(8,128)} async-done(((f32[768,3072]{1,0:T(8,128)}), f32[48,3072]{1,0:T(8,128)}) %reduce-scatter.15.cloned.1.call-update) | async-done | bytes 589840 | tf_op jit(solution)/shard_map/reduce_scatter | solution.py:354
  868.1 113.8 %reduce-scatter.17.cloned.1.call-done = f32[192,768]{1,0:T(8,128)} async-done(((f32[3072,768]{1,0:T(8,128)}), f32[192,768]{1,0:T(8,128)}) %reduce-scatter.17.cloned.1.call-update) | async-done | bytes 589840 | tf_op jit(solution)/shard_map/reduce_scatter | solution.py:355
  984.4 56.8 %reduce-scatter.21.cloned.1.call-done = f32[48,2]{1,0:T(8,128)} async-done(((f32[768,2]{1,0:T(8,128)}), f32[48,2]{1,0:T(8,128)}) %reduce-scatter.21.cloned.1.call-update) | async-done | bytes 400
  1050.6 49.7 %reduce-scatter.23.cloned.1.call-done = f32[48,5]{1,0:T(8,128)} async-done(((f32[768,5]{1,0:T(8,128)}), f32[48,5]{1,0:T(8,128)}) %reduce-scatter.23.cloned.1.call-update) | async-done | bytes 976
  1111.7 55.8 %all-reduce.8.cloned.1.call-done = (bf16[1,48,2304]{2,1,0:T(8,128)(2,1)}, bf16[1,48,2304]{1,2,0:T(8,128)(2,1)}, bf16[1,48,768]{2,1,0:T(8,128)(2,1)}, bf16[1,48,7...) async-done(((bf16[1,48,2304]{2,1,0:T(8,128)(2,1)}, ...) | async-done | bytes 1769488 | tf_op jit(solution)/shard_map/psum | solution.py:342
  (476 shorter events, 311.8 us)
Async XLA Ops:
  7.2 54.1 %all-gather.25.cloned.1.call-start = ((), (), s32[]{:S(2)}) async-start(), calls=%async_computation.13 | async-start | bytes 3760128 | tf_op jit(solution)/shard_map/all_gather | solution.py:266
  9.1 324.7 %all-gather.27.cloned.1.call-start = ((), (), s32[]{:S(2)}) async-start(), calls=%async_computation.14 | async-start | bytes 1253376 | tf_op jit(solution)/shard_map/all_gather | solution.py:267
  10.8 328.6 %all-gather.29.cloned.1.call-start = ((), (), s32[]{:S(2)}) async-start(), calls=%async_computation.15 | async-start | bytes 5013504 | tf_op jit(solution)/shard_map/all_gather | solution.py:268
  12.9 362.9 %all-gather.31.cloned.1.call-start = ((), (), s32[]{:S(2)}) async-start(), calls=%async_computation.16 | async-start | bytes 5013504 | tf_op jit(solution)/shard_map/all_gather | solution.py:269
  13.8 393.8 %all-gather.33.cloned.1.call-start = ((), (), s32[]{:S(2)}) async-start(), calls=%async_computation.17 | async-start | bytes 3760128 | tf_op jit(solution)/shard_map/all_gather | solution.py:286
  14.4 397.4 %all-gather.35.cloned.1.call-start = ((), (), s32[]{:S(2)}) async-start(), calls=%async_computation.18 | async-start | bytes 1253376 | tf_op jit(solution)/shard_map/all_gather | solution.py:287
  15.0 398.9 %all-gather.37.cloned.1.call-start = ((), (), s32[]{:S(2)}) async-start(), calls=%async_computation.19 | async-start | bytes 5013504 | tf_op jit(solution)/shard_map/all_gather | solution.py:288
  53.0 322.8 %copy-start.72 = (f32[768]{0:T(1024)}, f32[768]{0:T(1024)S(1)}, u32[]{:S(2)}) copy-start(f32[768]{0:T(1024)S(1)} %get-tuple-element.99) | copy-start | bytes 9220
  81.3 76.9 %all-to-all-start = ((bf16[3,1024,768]{1,0,2:T(4,128)(2,1)}), bf16[3,1024,768]{1,0,2:T(4,128)(2,1)}, u32[]{:S(2)}, u32[]{:S(2)}) async-start(bf16[3,1024,768]{1,0,2:T(4,128)(2,1)} %copy.112), calls=%async_computation | async-start | bytes 12582912 | tf_op jit(solution)/shard_map/all_to_all | solution.py:98
  87.8 334.6 %all-gather.39.cloned.1.call-start = ((), (), s32[]{:S(2)}) async-start(), calls=%async_computation.20 | async-start | bytes 5013504 | tf_op jit(solution)/shard_map/all_gather | solution.py:289
  133.8 273.5 %copy-start.109 = (s32[128]{0:T(128)}, s32[128]{0:T(128)S(1)}, u32[]{:S(2)}) copy-start(s32[128]{0:T(128)S(1)} %convert_reduce_fusion.9) | copy-start | bytes 1540
  138.4 237.4 %copy-start.64 = (f32[768]{0:T(1024)}, f32[768]{0:T(1024)S(1)}, u32[]{:S(2)}) copy-start(f32[768]{0:T(1024)S(1)} %get-tuple-element.96) | copy-start | bytes 9220
  138.4 247.3 %copy-start.66 = (f32[768]{0:T(1024)}, f32[768]{0:T(1024)S(1)}, u32[]{:S(2)}) copy-start(f32[768]{0:T(1024)S(1)} %get-tuple-element.95) | copy-start | bytes 9220
  193.4 140.5 %all-to-all-start.1 = ((bf16[2,1024,384]{1,2,0:T(8,128)(2,1)}), bf16[2,1024,384]{1,2,0:T(8,128)(2,1)S(1)}, u32[]{:S(2)}, u32[]{:S(2)}) async-start(bf16[2,1024,384]{1,2,0:T(8,128)(2,1)} %copy.119), calls=%async_computation.1 | async-start | bytes 3145728 | tf_op jit(solution)/shard_map/all_to_all | solution.py:104
  485.0 23.8 %all-to-all-start.2 = ((bf16[1024,2,384]{0,2,1:T(8,128)(2,1)}), bf16[1024,2,384]{0,2,1:T(8,128)(2,1)S(1)}, u32[]{:S(2)}, u32[]{:S(2)}) async-start(bf16[1024,2,384]{0,2,1:T(8,128)(2,1)} %bitcast.306), calls=%async_computation.2 | async-start | bytes 3145728 | tf_op jit(solution)/shard_map/all_to_all | solution.py:110
  488.8 280.3 %reduce-scatter.13.cloned.1.call-start = ((), (), s32[]{:S(2)}) async-start(), calls=%async_computation.10 | async-start | bytes 2506752 | tf_op jit(solution)/shard_map/reduce_scatter | solution.py:353
  493.6 277.4 %reduce-scatter.19.cloned.1.call-start = ((), (), s32[]{:S(2)}) async-start(), calls=%async_computation.21 | async-start | bytes 7520256
  663.7 202.6 %reduce-scatter.15.cloned.1.call-start = ((), (), s32[]{:S(2)}) async-start(), calls=%async_computation.11 | async-start | bytes 10027008 | tf_op jit(solution)/shard_map/reduce_scatter | solution.py:354
  676.5 305.3 %reduce-scatter.17.cloned.1.call-start = ((), (), s32[]{:S(2)}) async-start(), calls=%async_computation.12 | async-start | bytes 10027008 | tf_op jit(solution)/shard_map/reduce_scatter | solution.py:355
  689.7 351.5 %reduce-scatter.21.cloned.1.call-start = ((), (), s32[]{:S(2)}) async-start(), calls=%async_computation.22 | async-start | bytes 417792
  765.9 334.4 %reduce-scatter.23.cloned.1.call-start = ((), (), s32[]{:S(2)}) async-start(), calls=%async_computation.23 | async-start | bytes 417792
  767.8 216.1 %copy-start.51 = (f32[128,768]{1,0:T(8,128)S(1)}, f32[128,768]{1,0:T(8,128)}, u32[]{:S(2)}) copy-start(f32[128,768]{1,0:T(8,128)} %copy-done.50) | copy-start | bytes 1179652
  768.8 273.3 %copy-start.31 = (f32[1024,768]{1,0:T(8,128)S(1)}, f32[1024,768]{1,0:T(8,128)}, u32[]{:S(2)}) copy-start(f32[1024,768]{1,0:T(8,128)} %copy-done.30) | copy-start | bytes 9437188
  768.8 398.7 %all-reduce.8.cloned.1.call-start = ((), (), s32[]{:S(2)}) async-start(), calls=%async_computation.24 | async-start | bytes 4276224 | tf_op jit(solution)/shard_map/psum | solution.py:342
  (116 other events, 1994.0 us)
Sparse Core Ops, SparseCore 0:
  10.9 50.4 all-gather.24
  63.6 37.5 all-gather.26
  104.0 52.5 all-gather.28
  159.3 51.9 all-gather.30
  213.4 46.2 all-gather.32
  261.9 38.5 all-gather.34
  303.3 52.3 all-gather.36
  358.5 53.4 all-gather.38
  493.7 60.8 reduce-scatter.12
  663.8 87.2 reduce-scatter.18
  755.2 111.0 reduce-scatter.14
  870.8 111.0 reduce-scatter.16
  986.0 55.2 reduce-scatter.20
  1045.6 54.6 reduce-scatter.22
  1103.4 64.0 all-reduce.7
where the time goes:
time: 1190 us; the launch traced here: 1180 us
  waiting for transfers between devices  415 us (35%)
  blocking collectives  345 us (29%)
  matrix products  188 us (16%)
  local copies, waits for them, and re-layouts  157 us (13%)
  other arithmetic  44.3 us (4%)
  between operations  17.4 us (1%)
  starting transfers between devices  14.8 us (1%)
    unnamed x2, blocking collectives  120 us
    reduce_scatter x1, waiting for transfers between devices, body(): lax.psum_scatter(seg_grads[3], 'shard', scatter_dimension=0, tiled=True)  114 us
    unnamed x18, waiting for transfers between devices  109 us
    reduce_scatter x1, waiting for transfers between devices, body(): lax.psum_scatter(seg_grads[2], 'shard', scatter_dimension=0, tiled=True)  93.1 us
    all_to_all x1, blocking collectives, segment_back(): lax.all_to_all(stacked, 'seq', split_axis=1, concat_axis=2, tiled=True)  74.2 us
    psum x1, waiting for transfers between devices, body(): lax.psum(cross_terms[0].astype(jnp.bfloat16), 'seq').astype(jnp.float32)  55.8 us
    dot_general x8, matrix products, times_transposed(): lax.dot_general(left_side, right_side, (((1,), (1,)), ((), ())), preferre...  47.9 us
    dot_general x2, matrix products, block_forward(): jnp.dot(first_low, up_full, preferred_element_type=jnp.float32)  44.8 us
  transfers between devices with their start and end apart: 18, of which 8 were waited for; matrix products, arithmetic and copies ran while one was open for 26% of the time, Pallas kernels for 0%

commit v1 on v0

v1 whole, which is shorter than its diff:
```python
from functools import partial

import jax
import jax.numpy as jnp
from jax import lax
from jax.experimental import pallas as pl
from jax.experimental.pallas import tpu as pltpu
from jax.sharding import PartitionSpec as P

HEAD = 64
SEG = 128
EPSILON = 1e-05
MASKED = -1e30
BF = jnp.bfloat16
F32 = jnp.float32
TILE = 256
VMEM_LIMIT = 60 * 1024 * 1024

GAIN1, GAIN2, BIAS_V, BIAS_O, BIAS_D, SHIFT1, SHIFT2, UP0 = 0, 1, 2, 3, 4, 5, 6, 7
VEC_ROWS = 16


def dot_nn(a, b):
    return lax.dot_general(a, b, (((1,), (0,)), ((), ())), preferred_element_type=F32)


def dot_nt(a, b):
    return lax.dot_general(a, b, (((1,), (1,)), ((), ())), preferred_element_type=F32)


def dot_tn(a, b):
    return lax.dot_general(a, b, (((0,), (0,)), ((), ())), preferred_element_type=F32)


def row_mean(x):
    return jnp.mean(x, axis=-1, keepdims=True)


def col_sum(x):
    return jnp.sum(x.astype(F32), axis=0, keepdims=True)


def norm_rows(z):
    centred = z - row_mean(z)
    inverse = lax.rsqrt(row_mean(centred * centred) + EPSILON)
    return centred * inverse, inverse


def norm_back(scaled, normed, inverse):
    return inverse * (scaled - row_mean(scaled) - normed * row_mean(scaled * normed))


def gelu_both(u):
    phi = 0.5 + 0.5 * lax.erf(u * (2.0**-0.5))
    return u * phi, phi + u * jnp.exp(-0.5 * u * u) * 0.3989422804014327


def halves(pair):
    lane = lax.broadcasted_iota(jnp.int32, pair.shape, 1)
    zero = jnp.zeros_like(pair)
    return jnp.concatenate([jnp.where(lane < HEAD, pair, zero), jnp.where(lane < HEAD, zero, pair)], axis=0)


def side_by_side(stacked):
    rows = stacked.shape[0] // 2
    return jnp.concatenate([stacked[:rows], stacked[rows:]], axis=1)


def pair_forward(q, k, v, allowed):
    scores = dot_nt(halves(q), k) * (HEAD**-0.5)
    if allowed is not None:
        scores = jnp.where(allowed, scores, MASKED)
    top = jnp.max(scores, axis=-1, keepdims=True)
    powers = jnp.exp(scores - top)
    weights = (powers / jnp.sum(powers, axis=-1, keepdims=True)).astype(BF)
    return weights, dot_nn(side_by_side(weights), halves(v)).astype(BF)


def pair_backward(q, k, v, weights, d_out):
    d_stack = halves(d_out)
    d_weights = dot_nt(d_stack, v)
    wide = weights.astype(F32)
    inner = jnp.sum(wide * d_weights, axis=-1, keepdims=True)
    d_scores = (wide * (d_weights - inner)).astype(BF)
    scale = HEAD**-0.5
    d_q = dot_nn(side_by_side(d_scores), halves(k)) * scale
    d_k = dot_tn(d_scores, halves(q)) * scale
    d_v = dot_tn(weights, d_stack)
    return d_q.astype(BF), d_k.astype(BF), d_v.astype(BF)


class Pieces:
    def __init__(self, entries, chunk):
        self.arrays = [e[0] for e in entries]
        self.meta = [(e[1], e[2], e[0].shape[0]) for e in entries]
        self.chunk = chunk

    def copies(self, refs, origin, sems, col, width, dst, group=1, block=0):
        out = []
        for n, (ref, (entry, first, rows)) in enumerate(zip(refs, self.meta)):
            start = pl.multiple_of((origin[entry] * group + block) * self.chunk + first, 16)
            out.append(pltpu.make_async_copy(ref.at[:, pl.ds(col, width)], dst.at[pl.ds(start, rows), :], sems.at[n]))
        return out


def start_all(copies):
    for c in copies:
        c.start()


def wait_all(copies):
    for c in copies:
        c.wait()


ANY = pl.BlockSpec(memory_space=pl.ANY)
SMEM = pl.BlockSpec(memory_space=pltpu.SMEM)


def whole(shape):
    return pl.BlockSpec(shape, lambda *i: (0,) * len(shape), pipeline_mode=pl.Buffered(1))


def whole_out(shape):
    return pl.BlockSpec(shape, lambda *i: (0,) * len(shape))


def tile(*shape):
    return pl.BlockSpec(shape, lambda i: (i,) + (0,) * (len(shape) - 1))


def cost(flops, nbytes):
    return pl.CostEstimate(flops=int(flops), bytes_accessed=int(nbytes), transcendentals=0)


def attention_kernel(pieces, width, *refs):
    n = len(pieces.arrays)
    origin, x_ref, vec = refs[0], refs[1], refs[2]
    srcs = refs[3 : 3 + n]
    qkv_ref, a_ref, o_ref, h_ref, hb_ref, n_ref, r_ref = refs[3 + n : 10 + n]
    wqkv, wout, sem1, sem2 = refs[10 + n :]

    @pl.when(pl.program_id(0) == 0)
    def _():
        first = pieces.copies(srcs, origin, sem1, 0, 3 * width, wqkv)
        second = pieces.copies(srcs, origin, sem2, 3 * width, width, wout)
        start_all(first)
        start_all(second)
        wait_all(first)
        wait_all(second)

    x = x_ref[...]
    qkv = dot_nn(x, wqkv[...])
    qkv_ref[:, : 2 * width] = qkv[:, : 2 * width].astype(BF)
    qkv_ref[:, 2 * width :] = (qkv[:, 2 * width :] + vec[BIAS_V : BIAS_V + 1, :]).astype(BF)
    for s in range(TILE // SEG):
        rows = pl.ds(s * SEG, SEG)
        for p in range(width // 128):
            q = qkv_ref[rows, pl.ds(p * 128, 128)]
            k = qkv_ref[rows, pl.ds(width + p * 128, 128)]
            v = qkv_ref[rows, pl.ds(2 * width + p * 128, 128)]
            weights, out = pair_forward(q, k, v, None)
            a_ref[s, p] = weights
            o_ref[rows, pl.ds(p * 128, 128)] = out
    z = x.astype(F32) + dot_nn(o_ref[...], wout[...]) + vec[BIAS_O : BIAS_O + 1, :]
    normed, inverse = norm_rows(z)
    h = normed * vec[GAIN1 : GAIN1 + 1, :] + vec[SHIFT1 : SHIFT1 + 1, :]
    h_ref[...] = h
    hb_ref[...] = h.astype(BF)
    n_ref[...] = normed.astype(BF)
    r_ref[...] = inverse


def attention_call(origin, x, vec, pieces):
    rows, width = x.shape
    n = len(pieces.arrays)
    segs = rows // SEG
    pairs = width // 128
    return pl.pallas_call(
        partial(attention_kernel, pieces, width),
        grid=(rows // TILE,),
        in_specs=[SMEM, tile(TILE, width), whole(vec.shape)] + [ANY] * n,
        out_specs=[
            tile(TILE, 3 * width),
            tile(TILE // SEG, pairs, 2 * SEG, SEG),
            tile(TILE, width),
            tile(TILE, width),
            tile(TILE, width),
            tile(TILE, width),
            tile(TILE, 1),
        ],
        out_shape=[
            jax.ShapeDtypeStruct((rows, 3 * width), BF),
            jax.ShapeDtypeStruct((segs, pairs, 2 * SEG, SEG), BF),
            jax.ShapeDtypeStruct((rows, width), BF),
            jax.ShapeDtypeStruct((rows, width), F32),
            jax.ShapeDtypeStruct((rows, width), BF),
            jax.ShapeDtypeStruct((rows, width), BF),
            jax.ShapeDtypeStruct((rows, 1), F32),
        ],
        scratch_shapes=[
            pltpu.VMEM((width, 3 * width), BF),
            pltpu.VMEM((width, width), BF),
            pltpu.SemaphoreType.DMA((n,)),
            pltpu.SemaphoreType.DMA((n,)),
        ],
        compiler_params=pltpu.CompilerParams(vmem_limit_bytes=VMEM_LIMIT),
        cost_estimate=cost(2 * rows * width * 5 * width, 16 * rows * width),
        name="segment_attention",
    )(origin, x, vec, *pieces.arrays)


def up_down_copies(pieces, srcs, origin, sem_up, sem_down, width, ff, wup, wdown):
    ups = pieces.copies(srcs, origin, sem_up, 0, ff, wup)
    downs = []
    group = ff // width
    for j in range(group):
        downs += pieces.copies(srcs, origin, sem_down.at[j], ff + j * width, width, wdown, group, j)
    return ups, downs


def feed_kernel(pieces, width, ff, *refs):
    n = len(pieces.arrays)
    origin, h_ref, c_ref, o_ref, n_ref, r_ref, vec, upb = refs[:8]
    srcs = refs[8 : 8 + n]
    y_ref, g_ref, gp_ref, dz_ref, pay_ref, sums_ref = refs[8 + n : 14 + n]
    wup, wdown, sem_up, sem_down = refs[14 + n :]
    step = pl.program_id(0)

    @pl.when(step == 0)
    def _():
        ups, downs = up_down_copies(pieces, srcs, origin, sem_up, sem_down, width, ff, wup, wdown)
        start_all(ups)
        start_all(downs)
        wait_all(ups)
        wait_all(downs)
        sums_ref[...] = jnp.zeros_like(sums_ref)

    h = h_ref[...]
    hb = h.astype(BF)
    block = 512
    total = jnp.zeros((TILE, width), F32)
    u = dot_nn(hb, wup[:, :block]) + upb[:, :block]
    for j in range(ff // block):
        cols = slice(j * block, (j + 1) * block)
        if (j + 1) * block < ff:
            later = slice((j + 1) * block, (j + 2) * block)
            u_next = dot_nn(hb, wup[:, later]) + upb[:, later]
        active, slope = gelu_both(u)
        active = active.astype(BF)
        g_ref[:, cols] = active
        gp_ref[:, cols] = slope.astype(BF)
        total = total + dot_nn(active, wdown[cols, :])
        u = u_next
    normed, inverse = norm_rows(h + total + vec[BIAS_D : BIAS_D + 1, :])
    gain = vec[GAIN2 : GAIN2 + 1, :]
    y = normed * gain + vec[SHIFT2 : SHIFT2 + 1, :]
    y_ref[...] = y.astype(BF)
    row = lax.broadcasted_iota(jnp.int32, (TILE, 1), 0)
    dy = jnp.where(row % SEG == 0, 0.0, c_ref[...].astype(F32))
    dz = norm_back(dy * gain, normed, inverse)
    dz_ref[...] = dz
    sums_ref[0:1, :] += col_sum(dy * normed)
    sums_ref[1:2, :] += col_sum(dy)
    sums_ref[2:3, :] += col_sum(dz.astype(BF))
    lane = lax.broadcasted_iota(jnp.int32, (1, 128), 1)
    for s in range(TILE // SEG):
        here = slice(s * SEG, s * SEG + 1)
        at = slice(s, s + 1)
        pay_ref[0, at, 0:width] = y[here]
        pay_ref[0, at, width : 2 * width] = h[here]
        pay_ref[0, at, 2 * width : 3 * width] = o_ref[s * SEG : s * SEG + 16, :].astype(F32)[:1]
        pay_ref[0, at, 3 * width : 4 * width] = n_ref[s * SEG : s * SEG + 16, :].astype(F32)[:1]
        r = r_ref[here]
        r_high = r.astype(BF).astype(F32)
        pay_ref[0, at, 4 * width :] = jnp.where(lane == 0, r_high, jnp.where(lane == 1, r - r_high, 0.0))


def feed_call(origin, h, cot, o, n1, r1, vec, upb, pieces, ff):
    rows, width = h.shape
    n = len(pieces.arrays)
    group = ff // width
    return pl.pallas_call(
        partial(feed_kernel, pieces, width, ff),
        grid=(rows // TILE,),
        in_specs=[
            SMEM,
            tile(TILE, width),
            tile(TILE, width),
            tile(TILE, width),
            tile(TILE, width),
            tile(TILE, 1),
            whole(vec.shape),
            whole(upb.shape),
        ]
        + [ANY] * n,
        out_specs=[
            tile(TILE, width),
            tile(TILE, ff),
            tile(TILE, ff),
            tile(TILE, width),
            pl.BlockSpec((1, TILE // SEG, 4 * width + 128), lambda i: (i, 0, 0)),
            whole_out((8, width)),
        ],
        out_shape=[
            jax.ShapeDtypeStruct((rows, width), BF),
            jax.ShapeDtypeStruct((rows, ff), BF),
            jax.ShapeDtypeStruct((rows, ff), BF),
            jax.ShapeDtypeStruct((rows, width), F32),
            jax.ShapeDtypeStruct((rows // TILE, TILE // SEG, 4 * width + 128), F32),
            jax.ShapeDtypeStruct((8, width), F32),
        ],
        scratch_shapes=[
            pltpu.VMEM((width, ff), BF),
            pltpu.VMEM((ff, width), BF),
            pltpu.SemaphoreType.DMA((n,)),
            pltpu.SemaphoreType.DMA((group, n)),
        ],
        compiler_params=pltpu.CompilerParams(vmem_limit_bytes=VMEM_LIMIT),
        cost_estimate=cost(4 * rows * width * ff, 4 * rows * ff),
        name="segment_feed",
    )(origin, h, cot, o, n1, r1, vec, upb, *pieces.arrays)


def feed_back_kernel(pieces, pieces_out, width, ff, *refs):
    n, m = len(pieces.arrays), len(pieces_out.arrays)
    origin, dz_ref, gp_ref, n_ref, r_ref, vec = refs[:6]
    srcs = refs[6 : 6 + n]
    srcs_out = refs[6 + n : 6 + n + m]
    dm_ref, du_ref, dz1_ref, db_ref, do_ref, sums_ref, upsum_ref = refs[6 + n + m : 13 + n + m]
    wup, wdown, wout, sem_up, sem_down, sem_out = refs[13 + n + m :]

    @pl.when(pl.program_id(0) == 0)
    def _():
        ups, downs = up_down_copies(pieces, srcs, origin, sem_up, sem_down, width, ff, wup, wdown)
        outs = pieces_out.copies(srcs_out, origin, sem_out, 3 * width, width, wout)
        start_all(downs)
        start_all(ups)
        start_all(outs)
        wait_all(downs)
        wait_all(ups)
        wait_all(outs)
        sums_ref[...] = jnp.zeros_like(sums_ref)
        upsum_ref[...] = jnp.zeros_like(upsum_ref)

    dz = dz_ref[...]
    dm = dz.astype(BF)
    dm_ref[...] = dm
    block = 512
    total = dz
    dg = dot_nt(dm, wdown[:block, :])
    for j in range(ff // block):
        cols = slice(j * block, (j + 1) * block)
        if (j + 1) * block < ff:
            dg_next = dot_nt(dm, wdown[(j + 1) * block : (j + 2) * block, :])
        du = (dg * gp_ref[:, cols].astype(F32)).astype(BF)
        du_ref[:, cols] = du
        upsum_ref[0:1, cols] += col_sum(du)
        total = total + dot_nt(du, wup[:, cols])
        dg = dg_next
    normed = n_ref[...].astype(F32)
    dz1 = norm_back(total * vec[GAIN1 : GAIN1 + 1, :], normed, r_ref[...])
    dz1_ref[...] = dz1
    db = dz1.astype(BF)
    db_ref[...] = db
    do_ref[...] = dot_nt(db, wout[...]).astype(BF)
    sums_ref[0:1, :] += col_sum(total * normed)
    sums_ref[1:2, :] += col_sum(total)
    sums_ref[2:3, :] += col_sum(db)


def feed_back_call(origin, dz, gp, n1, r1, vec, pieces, pieces_out):
    rows, width = dz.shape
    ff = gp.shape[1]
    n, m = len(pieces.arrays), len(pieces_out.arrays)
    return pl.pallas_call(
        partial(feed_back_kernel, pieces, pieces_out, width, ff),
        grid=(rows // TILE,),
        in_specs=[SMEM, tile(TILE, width), tile(TILE, ff), tile(TILE, width), tile(TILE, 1), whole(vec.shape)]
        + [ANY] * (n + m),
        out_specs=[
            tile(TILE, width),
            tile(TILE, ff),
            tile(TILE, width),
            tile(TILE, width),
            tile(TILE, width),
            whole_out((8, width)),
            whole_out((8, ff)),
        ],
        out_shape=[
            jax.ShapeDtypeStruct((rows, width), BF),
            jax.ShapeDtypeStruct((rows, ff), BF),
            jax.ShapeDtypeStruct((rows, width), F32),
            jax.ShapeDtypeStruct((rows, width), BF),
            jax.ShapeDtypeStruct((rows, width), BF),
            jax.ShapeDtypeStruct((8, width), F32),
            jax.ShapeDtypeStruct((8, ff), F32),
        ],
        scratch_shapes=[
            pltpu.VMEM((width, ff), BF),
            pltpu.VMEM((ff, width), BF),
            pltpu.VMEM((width, width), BF),
            pltpu.SemaphoreType.DMA((n,)),
            pltpu.SemaphoreType.DMA((ff // width, n)),
            pltpu.SemaphoreType.DMA((m,)),
        ],
        compiler_params=pltpu.CompilerParams(vmem_limit_bytes=VMEM_LIMIT),
        cost_estimate=cost(4 * rows * width * ff + 2 * rows * width * width, 4 * rows * ff),
        name="segment_feed_back",
    )(origin, dz, gp, n1, r1, vec, *pieces.arrays, *pieces_out.arrays)


class Slots:
    def __init__(self, chips, chunk, both):
        self.chips, self.chunk, self.both = chips, chunk, both

    def shapes(self, cols):
        s = jax.ShapeDtypeStruct((self.chips, self.chunk, cols), BF)
        return [s, s] if self.both else [s]

    def store(self, table, outs, source, rows_first, rows, chunk_of, col, width):
        pass


def grads_kernel(chips, cores, chunk, width, ff, *refs):
    table, g_ref, dm_ref, du_ref, hb_ref, o_ref, db_ref = refs[:7]
    outs = refs[7 : 7 + cores]
    scratch = refs[7 + cores]
    step = pl.program_id(0)
    group = ff // width
    core = table[chips]

    def spread(first_device, devices, blocks, col):
        for q in range(devices // cores):
            slot = table[first_device // cores + q]
            for c in range(cores):
                device = q * cores + (jnp.bitwise_xor(core, c) if cores > 1 else 0)
                for b in range(blocks):
                    start = pl.multiple_of((device * blocks + b) * chunk, 16)
                    outs[c][slot, :, pl.ds(col + b * width, width)] = scratch[pl.ds(start, chunk), :].astype(BF)

    per = chips * cores // group if chips * cores >= group else 1
    for j in range(group):

        @pl.when(step == j)
        def _(j=j):
            scratch[...] = dot_tn(g_ref[...], dm_ref[...])
            if chips * cores >= group:
                spread(j * per, per, group, ff)
            else:
                outs[0][0, :, pl.ds(ff + j * width, width)] = scratch[...].astype(BF)

        @pl.when(step == group + j)
        def _(j=j):
            scratch[...] = dot_tn(hb_ref[...], du_ref[...])
            spread(0, chips * cores, 1, j * width)

    @pl.when(step == 2 * group)
    def _():
        scratch[...] = dot_tn(o_ref[...], db_ref[...])
        spread(0, chips * cores, 1, 2 * ff)


def grads_call(table, g, dm, du, hb, o, db, chips, cores, chunk):
    rows, ff = g.shape
    width = dm.shape[1]
    group = ff // width
    cols = 2 * ff + width
    return pl.pallas_call(
        partial(grads_kernel, chips, cores, chunk, width, ff),
        grid=(2 * group + 1,),
        in_specs=[
            SMEM,
            pl.BlockSpec((rows, width), lambda i: (0, jnp.minimum(i, group - 1))),
            whole((rows, width)),
            pl.BlockSpec((rows, width), lambda i: (0, jnp.clip(i - group, 0, group - 1))),
            whole((rows, width)),
            whole((rows, width)),
            whole((rows, width)),
        ],
        out_specs=[pl.BlockSpec((chips, chunk, cols), lambda i: (0, 0, 0), pipeline_mode=pl.Buffered(1))] * cores,
        out_shape=[jax.ShapeDtypeStruct((chips, chunk, cols), BF)] * cores,
        scratch_shapes=[pltpu.VMEM((width, width), F32)],
        compiler_params=pltpu.CompilerParams(vmem_limit_bytes=VMEM_LIMIT),
        cost_estimate=cost(2 * rows * width * cols, 4 * rows * ff + 4 * width * cols),
        name="segment_grads",
    )(table, g, dm, du, hb, o, db)


def attention_back_kernel(pieces, chips, cores, chunk, width, *refs):
    n = len(pieces.arrays)
    origin, table, qkv_ref, a_ref, do_ref, dz_ref, x_ref, do_first, dz_first = refs[:9]
    srcs = refs[9 : 9 + n]
    dx_ref = refs[9 + n]
    sums_ref = refs[10 + n]
    outs = refs[11 + n : 11 + n + cores]
    wqkv, total, dqkv, d_o, d_z, sem = refs[11 + n + cores :]
    step = pl.program_id(0)

    @pl.when(step == 0)
    def _():
        copies = pieces.copies(srcs, origin, sem, 0, 3 * width, wqkv)
        start_all(copies)
        wait_all(copies)
        total[...] = jnp.zeros_like(total)
        sums_ref[...] = jnp.zeros_like(sums_ref)

    d_o[...] = do_ref[...].astype(F32)
    d_z[...] = dz_ref[...]
    for s in range(TILE // SEG):
        at = pl.ds(table[chips + 1] + step * (TILE // SEG) + s, 1)
        d_o[s * SEG : s * SEG + 1, :] = do_first[at, :]
        d_z[s * SEG : s * SEG + 1, :] = dz_first[at, :]
    for s in range(TILE // SEG):
        rows = pl.ds(s * SEG, SEG)
        for p in range(width // 128):
            q = qkv_ref[rows, pl.ds(p * 128, 128)]
            k = qkv_ref[rows, pl.ds(width + p * 128, 128)]
            v = qkv_ref[rows, pl.ds(2 * width + p * 128, 128)]
            d_out = d_o[rows, pl.ds(p * 128, 128)].astype(BF)
            d_q, d_k, d_v = pair_backward(q, k, v, a_ref[s, p], d_out)
            dqkv[rows, pl.ds(p * 128, 128)] = d_q
            dqkv[rows, pl.ds(width + p * 128, 128)] = d_k
            dqkv[rows, pl.ds(2 * width + p * 128, 128)] = d_v
    sums_ref[0:1, :] += col_sum(dqkv[:, 2 * width :])
    dx_ref[...] = (d_z[...] + dot_nt(dqkv[...], wqkv[...])).astype(BF)
    total[...] += dot_tn(x_ref[...], dqkv[...])

    @pl.when(step == pl.num_programs(0) - 1)
    def _():
        core = table[chips]
        for q in range(chips):
            slot = table[q]
            for c in range(cores):
                device = q * cores + (jnp.bitwise_xor(core, c) if cores > 1 else 0)
                start = pl.multiple_of(device * chunk, 16)
                outs[c][slot] = total[pl.ds(start, chunk), :].astype(BF)


def attention_back_call(origin, table, qkv, a, do, dz, x, do_first, dz_first, pieces, chips, cores, chunk):
    rows, width = x.shape
    n = len(pieces.arrays)
    pairs = width // 128
    return pl.pallas_call(
        partial(attention_back_kernel, pieces, chips, cores, chunk, width),
        grid=(rows // TILE,),
        in_specs=[
            SMEM,
            SMEM,
            tile(TILE, 3 * width),
            tile(TILE // SEG, pairs, 2 * SEG, SEG),
            tile(TILE, width),
            tile(TILE, width),
            tile(TILE, width),
            whole(do_first.shape),
            whole(dz_first.shape),
        ]
        + [ANY] * n,
        out_specs=[tile(TILE, width), whole_out((8, width))]
        + [pl.BlockSpec((chips, chunk, 3 * width), lambda i: (0, 0, 0), pipeline_mode=pl.Buffered(1))] * cores,
        out_shape=[jax.ShapeDtypeStruct((rows, width), BF), jax.ShapeDtypeStruct((8, width), F32)]
        + [jax.ShapeDtypeStruct((chips, chunk, 3 * width), BF)] * cores,
        scratch_shapes=[
            pltpu.VMEM((width, 3 * width), BF),
            pltpu.VMEM((width, 3 * width), F32),
            pltpu.VMEM((TILE, 3 * width), BF),
            pltpu.VMEM((TILE, width), F32),
            pltpu.VMEM((TILE, width), F32),
            pltpu.SemaphoreType.DMA((n,)),
        ],
        compiler_params=pltpu.CompilerParams(vmem_limit_bytes=VMEM_LIMIT),
        cost_estimate=cost(2 * rows * width * 8 * width, 20 * rows * width),
        name="segment_attention_back",
    )(origin, table, qkv, a, do, dz, x, do_first, dz_first, *pieces.arrays)


def one_hot(rows, cols, base):
    r = lax.broadcasted_iota(jnp.int32, (rows, cols), 0)
    c = lax.broadcasted_iota(jnp.int32, (rows, cols), 1)
    return (r == c + base).astype(F32).astype(BF)


def own_cols(values, base, cols):
    return dot_nn(values.astype(BF), one_hot(values.shape[1], cols, base)).astype(BF)


def few_feed_forward(hb, h, vec, upb, wup, wdown, g_ref, gp_ref, ff):
    block = 512
    total = jnp.zeros(h.shape, F32)
    for j in range(ff // block):
        cols = slice(j * block, (j + 1) * block)
        active, slope = gelu_both(dot_nn(hb, wup[:, cols]) + upb[:, cols])
        active = active.astype(BF)
        g_ref[:, cols] = active
        gp_ref[:, cols] = slope.astype(BF)
        total = total + dot_nn(active, wdown[cols, :])
    return norm_rows(h + total + vec[BIAS_D : BIAS_D + 1, :])


def few_feed_backward(dy, n2, r2, n1, r1, hb, o, vec, wup, wdown, wout, g_ref, gp_ref, me, chunk, ff, outs):
    gup_ref, gdown_ref, gout_ref, sums_ref, upsum_ref = outs
    block = 512
    group = ff // hb.shape[1]
    base = me * chunk
    dz = norm_back(dy * vec[GAIN2 : GAIN2 + 1, :], n2, r2)
    dm = dz.astype(BF)
    total = dz
    own_h = own_cols(hb, base, chunk)
    own_g = jnp.zeros((hb.shape[0], group * chunk), F32)
    own_up = jnp.zeros((8, group * chunk), F32)
    for j in range(ff // block):
        cols = slice(j * block, (j + 1) * block)
        du = (dot_nt(dm, wdown[cols, :]) * gp_ref[:, cols].astype(F32)).astype(BF)
        total = total + dot_nt(du, wup[:, cols])
        gup_ref[:, cols] = dot_tn(own_h, du).astype(BF)
        chosen = one_hot(block, group * chunk, base * group - j * block)
        own_g = own_g + dot_nn(g_ref[:, cols], chosen)
        own_up = own_up + dot_nn(jnp.broadcast_to(col_sum(du), (8, block)).astype(BF), chosen)
    gdown_ref[...] = dot_tn(own_g.astype(BF), dm).astype(BF)
    upsum_ref[...] = own_up
    dz1 = norm_back(total * vec[GAIN1 : GAIN1 + 1, :], n1, r1)
    db = dz1.astype(BF)
    gout_ref[...] = dot_tn(own_cols(o, base, chunk), db).astype(BF)
    do = dot_nt(db, wout[...])
    sums = [col_sum(total * n1), col_sum(dy * n2), None, col_sum(db), col_sum(dm), col_sum(total), col_sum(dy)]
    sums[2] = jnp.zeros_like(sums[0])
    stacked = jnp.concatenate(sums + [jnp.zeros_like(sums[0])], axis=0)
    sums_ref[...] = dot_nn(stacked.astype(BF), one_hot(hb.shape[1], chunk, base))
    return dz1, do


def cross_kernel(pa, pb, width, ff, chunk, places_n, *refs):
    na, nb = len(pa.arrays), len(pb.arrays)
    origin, table, heads_ref, grad_ref, doc_col, doc_row, tab_ref, vec, upb = refs[:9]
    srca = refs[9 : 9 + na]
    srcb = refs[9 + na : 9 + na + nb]
    base_o = 9 + na + nb
    out_ref, dx_ref, gqkv_ref, gout_ref, gup_ref, gdown_ref, sums_ref, upsum_ref, gtab_ref = refs[base_o : base_o + 9]
    wqkv, wout, wup, wdown, qkv, a_ref, o_s, d_s, g_ref, gp_ref, sem_a, sem_o, sem_up, sem_down = refs[base_o + 9 :]
    rows = heads_ref.shape[0]
    me = table[0]
    ca = pa.copies(srca, origin, sem_a, 0, 3 * width, wqkv)
    co = pa.copies(srca, origin, sem_o, 3 * width, width, wout)
    ups, downs = up_down_copies(pb, srcb, origin, sem_up, sem_down, width, ff, wup, wdown)
    start_all(ca)
    start_all(co)
    start_all(ups)
    start_all(downs)
    same = doc_col[...] == doc_row[...]
    earlier = lax.broadcasted_iota(jnp.int32, (rows, rows), 0) > lax.broadcasted_iota(jnp.int32, (rows, rows), 1)
    position = jnp.sum(jnp.where(same & earlier, 1.0, 0.0), axis=1, keepdims=True)
    slot = lax.broadcasted_iota(jnp.int32, (rows, places_n), 1).astype(F32)
    lookup = (slot == position).astype(F32).astype(BF)
    entry = heads_ref[...].astype(F32) + dot_nn(lookup, tab_ref[...].astype(BF))
    low = entry.astype(BF)
    allowed = jnp.concatenate([same, same], axis=0)
    wait_all(ca)
    proj = dot_nn(low, wqkv[...])
    qkv[:, : 2 * width] = proj[:, : 2 * width].astype(BF)
    qkv[:, 2 * width :] = (proj[:, 2 * width :] + vec[BIAS_V : BIAS_V + 1, :]).astype(BF)
    for p in range(width // 128):
        q = qkv[:, p * 128 : (p + 1) * 128]
        k = qkv[:, width + p * 128 : width + (p + 1) * 128]
        v = qkv[:, 2 * width + p * 128 : 2 * width + (p + 1) * 128]
        weights, out = pair_forward(q, k, v, allowed)
        a_ref[p] = weights
        o_s[:, p * 128 : (p + 1) * 128] = out
    wait_all(co)
    o = o_s[...]
    n1, r1 = norm_rows(entry + dot_nn(o, wout[...]) + vec[BIAS_O : BIAS_O + 1, :])
    h = n1 * vec[GAIN1 : GAIN1 + 1, :] + vec[SHIFT1 : SHIFT1 + 1, :]
    hb = h.astype(BF)
    wait_all(ups)
    wait_all(downs)
    n2, r2 = few_feed_forward(hb, h, vec, upb, wup, wdown, g_ref, gp_ref, ff)
    out_ref[...] = n2 * vec[GAIN2 : GAIN2 + 1, :] + vec[SHIFT2 : SHIFT2 + 1, :]
    dy = grad_ref[...].astype(F32)
    outs = (gup_ref, gdown_ref, gout_ref, sums_ref, upsum_ref)
    dz1, do = few_feed_backward(dy, n2, r2, n1, r1, hb, o, vec, wup, wdown, wout, g_ref, gp_ref, me, chunk, ff, outs)
    do = do.astype(BF)
    for p in range(width // 128):
        q = qkv[:, p * 128 : (p + 1) * 128]
        k = qkv[:, width + p * 128 : width + (p + 1) * 128]
        v = qkv[:, 2 * width + p * 128 : 2 * width + (p + 1) * 128]
        d_q, d_k, d_v = pair_backward(q, k, v, a_ref[p], do[:, p * 128 : (p + 1) * 128])
        d_s[:, p * 128 : (p + 1) * 128] = d_q
        d_s[:, width + p * 128 : width + (p + 1) * 128] = d_k
        d_s[:, 2 * width + p * 128 : 2 * width + (p + 1) * 128] = d_v
    d_all = d_s[...]
    gqkv_ref[...] = dot_tn(own_cols(low, me * chunk, chunk), d_all).astype(BF)
    d_in = dz1 + dot_nt(d_all, wqkv[...])
    dx_ref[...] = d_in
    high = d_in.astype(BF)
    rest = (d_in - high.astype(F32)).astype(BF)
    gtab = dot_tn(lookup, high) + dot_tn(lookup, rest)
    pick = one_hot(width, chunk, me * chunk)
    gtab_ref[...] = dot_nn(gtab.astype(BF), pick)
    dv = jnp.broadcast_to(col_sum(d_all[:, 2 * width :]), (8, width)).astype(BF)
    row = lax.broadcasted_iota(jnp.int32, (8, chunk), 0)
    sums_ref[...] += jnp.where(row == 2, dot_nn(dv, pick), 0.0)


def cross_call(origin, table, heads, grad, docs, tab, vec, upb, pa, pb, ff, chunk):
    rows, width = heads.shape
    na, nb = len(pa.arrays), len(pb.arrays)
    group = ff // width
    pairs = width // 128
    full = pl.BlockSpec(memory_space=pltpu.VMEM)
    return pl.pallas_call(
        partial(cross_kernel, pa, pb, width, ff, chunk, tab.shape[0]),
        in_specs=[SMEM, SMEM] + [full] * 7 + [ANY] * (na + nb),
        out_specs=[full] * 9,
        out_shape=[
            jax.ShapeDtypeStruct((rows, width), F32),
            jax.ShapeDtypeStruct((rows, width), F32),
            jax.ShapeDtypeStruct((chunk, 3 * width), BF),
            jax.ShapeDtypeStruct((chunk, width), BF),
            jax.ShapeDtypeStruct((chunk, ff), BF),
            jax.ShapeDtypeStruct((group * chunk, width), BF),
            jax.ShapeDtypeStruct((8, chunk), F32),
            jax.ShapeDtypeStruct((8, group * chunk), F32),
            jax.ShapeDtypeStruct((tab.shape[0], chunk), F32),
        ],
        scratch_shapes=[
            pltpu.VMEM((width, 3 * width), BF),
            pltpu.VMEM((width, width), BF),
            pltpu.VMEM((width, ff), BF),
            pltpu.VMEM((ff, width), BF),
            pltpu.VMEM((rows, 3 * width), BF),
            pltpu.VMEM((pairs, 2 * rows, rows), BF),
            pltpu.VMEM((rows, width), BF),
            pltpu.VMEM((rows, 3 * width), BF),
            pltpu.VMEM((rows, ff), BF),
            pltpu.VMEM((rows, ff), BF),
            pltpu.SemaphoreType.DMA((na,)),
            pltpu.SemaphoreType.DMA((na,)),
            pltpu.SemaphoreType.DMA((nb,)),
            pltpu.SemaphoreType.DMA((group, nb)),
        ],
        compiler_params=pltpu.CompilerParams(vmem_limit_bytes=VMEM_LIMIT),
        cost_estimate=cost(16 * rows * width * ff, 20 * width * width),
        name="cross_block",
    )(origin, table, heads, grad, docs.reshape(rows, 1), docs.reshape(1, rows), tab, vec, upb, *pa.arrays, *pb.arrays)


def first_kernel(pa, pb, width, ff, chunk, *refs):
    na, nb = len(pa.arrays), len(pb.arrays)
    origin, table, pay_ref, dy_ref, vec, upb = refs[:6]
    srca = refs[6 : 6 + na]
    srcb = refs[6 + na : 6 + na + nb]
    base_o = 6 + na + nb
    dz1_ref, do_ref, gout_ref, gup_ref, gdown_ref, sums_ref, upsum_ref = refs[base_o : base_o + 7]
    wout, wup, wdown, g_ref, gp_ref, sem_o, sem_up, sem_down = refs[base_o + 7 :]
    me = table[0]
    co = pa.copies(srca, origin, sem_o, 3 * width, width, wout)
    ups, downs = up_down_copies(pb, srcb, origin, sem_up, sem_down, width, ff, wup, wdown)
    start_all(ups)
    start_all(downs)
    start_all(co)
    hb = pay_ref[:, width : 2 * width]
    o = pay_ref[:, 2 * width : 3 * width]
    n1 = pay_ref[:, 3 * width : 4 * width].astype(F32)
    r1 = jnp.sum(pay_ref[:, 4 * width :].astype(F32), axis=1, keepdims=True)
    wait_all(ups)
    wait_all(downs)
    wait_all(co)
    n2, r2 = few_feed_forward(hb, hb.astype(F32), vec, upb, wup, wdown, g_ref, gp_ref, ff)
    outs = (gup_ref, gdown_ref, gout_ref, sums_ref, upsum_ref)
    dz1, do = few_feed_backward(
        dy_ref[...], n2, r2, n1, r1, hb, o, vec, wup, wdown, wout, g_ref, gp_ref, me, chunk, ff, outs
    )
    dz1_ref[...] = dz1
    do_ref[...] = do


def first_call(origin, table, pay, dy, vec, upb, pa, pb, ff, chunk):
    rows, width = dy.shape
    na, nb = len(pa.arrays), len(pb.arrays)
    group = ff // width
    full = pl.BlockSpec(memory_space=pltpu.VMEM)
    return pl.pallas_call(
        partial(first_kernel, pa, pb, width, ff, chunk),
        in_specs=[SMEM, SMEM] + [full] * 4 + [ANY] * (na + nb),
        out_specs=[full] * 7,
        out_shape=[
            jax.ShapeDtypeStruct((rows, width), F32),
            jax.ShapeDtypeStruct((rows, width), F32),
            jax.ShapeDtypeStruct((chunk, width), BF),
            jax.ShapeDtypeStruct((chunk, ff), BF),
            jax.ShapeDtypeStruct((group * chunk, width), BF),
            jax.ShapeDtypeStruct((8, chunk), F32),
            jax.ShapeDtypeStruct((8, group * chunk), F32),
        ],
        scratch_shapes=[
            pltpu.VMEM((width, width), BF),
            pltpu.VMEM((width, ff), BF),
            pltpu.VMEM((ff, width), BF),
            pltpu.VMEM((rows, ff), BF),
            pltpu.VMEM((rows, ff), BF),
            pltpu.SemaphoreType.DMA((na,)),
            pltpu.SemaphoreType.DMA((nb,)),
            pltpu.SemaphoreType.DMA((group, nb)),
        ],
        compiler_params=pltpu.CompilerParams(vmem_limit_bytes=VMEM_LIMIT),
        cost_estimate=cost(14 * rows * width * ff, 15 * width * width),
        name="first_rows",
    )(origin, table, pay, dy, vec, upb, *pa.arrays, *pb.arrays)


class Ring:
    def __init__(self, shards):
        chips = shards // 2
        self.shards, self.chips = shards, chips
        self.order = list(range(0, chips, 2)) + list(range(chips - 1, 0, -2))
        self.place = {chip: i for i, chip in enumerate(self.order)}

    def shift(self, by):
        pairs = []
        for i, chip in enumerate(self.order):
            to = self.order[(i + by) % self.chips]
            pairs += [(2 * chip, 2 * to), (2 * chip + 1, 2 * to + 1)]
        return pairs

    def forward(self, x):
        return lax.ppermute(x, "shard", self.shift(1))

    def backward(self, x):
        return lax.ppermute(x, "shard", self.shift(-1))

    def sibling(self, x):
        return lax.ppermute(x, "shard", [(i, i ^ 1) for i in range(self.shards)])

    def origin_table(self):
        rows = []
        for d in range(self.shards):
            chip, core = d // 2, d % 2
            row = []
            for k in range(self.chips):
                other = self.order[(self.place[chip] - k) % self.chips]
                row += [2 * other + core, 2 * other + 1 - core]
            rows.append(row)
        return rows

    def slot_table(self):
        rows = []
        for d in range(self.shards):
            chip = d // 2
            rows.append([(self.place[q] - self.place[chip]) % self.chips for q in range(self.chips)] + [d % 2])
        return rows

    def gather(self, x):
        rows = x.shape[0]
        half = (rows // 32) * 16 or rows
        entries = [(x, 0, 0), (self.sibling(x), 1, 0)]
        ahead, behind = x, x
        for step in range(1, self.chips // 2):
            ahead, behind = self.forward(ahead), self.backward(behind)
            entries += [(ahead, 2 * step, 0), (self.sibling(ahead), 2 * step + 1, 0)]
            back = self.chips - step
            entries += [(behind, 2 * back, 0), (self.sibling(behind), 2 * back + 1, 0)]
        far = self.chips // 2
        last_a = self.forward(ahead[:half])
        entries += [(last_a, 2 * far, 0), (self.sibling(last_a), 2 * far + 1, 0)]
        if half < rows:
            last_b = self.backward(behind[half:])
            entries += [(last_b, 2 * far, half), (self.sibling(last_b), 2 * far + 1, half)]
        return Pieces(entries, rows)

    def reduce(self, own, other):
        mine = self.sibling(other)

        def local(k):
            return own[k % self.chips] + mine[k % self.chips]

        far = self.chips // 2
        half = (own.shape[1] // 32) * 16 or own.shape[1]
        start = local(far)
        ahead = self.forward(start[:half])
        behind = self.backward(start[half:]) if half < own.shape[1] else None
        edge = local(far - 1)
        ahead = jnp.concatenate([ahead + edge[:half], edge[half:]], axis=0) if behind is not None else ahead + edge
        edge = local(-(far - 1))
        behind = jnp.concatenate([edge[:half], behind + edge[half:]], axis=0) if behind is not None else edge
        for step in range(far - 1, 1, -1):
            ahead = self.forward(ahead) + local(step - 1)
            behind = self.backward(behind) + local(-(step - 1))
        return local(0) + self.forward(ahead) + self.backward(behind)


def swap_seq(x):
    return lax.ppermute(x, "seq", [(0, 1), (1, 0)])


def over_seq(x):
    low = x.astype(BF)
    return low.astype(F32) + swap_seq(low).astype(F32)


def sum_everywhere(x, shards):
    low = x.astype(BF)
    bit = 1
    while bit < shards:
        low = low + lax.ppermute(low, "shard", [(i, i ^ bit) for i in range(shards)])
        bit *= 2
    return low.astype(F32) + swap_seq(low).astype(F32)


def pack(qkv, out, up, down):
    chunk = qkv.shape[0]
    parts = [down[j * chunk : (j + 1) * chunk] for j in range(down.shape[0] // chunk)]
    return jnp.concatenate([qkv, out], axis=1), jnp.concatenate([up] + parts, axis=1)


def body(
    tokens,
    qkv_weight,
    out_weight,
    up_weight,
    down_weight,
    norm_gains,
    biases,
    up_bias,
    position_table,
    segment_docs,
    cotangent,
):
    shards = lax.axis_size("shard")
    me = lax.axis_index("shard")
    rows, width = tokens.shape
    segs = rows // SEG
    ff = up_weight.shape[2]
    group = ff // width
    own = width // shards
    docs = segment_docs[0]
    ringed = own % 16 == 0
    ring = Ring(shards)

    def vec_rows(b):
        return [norm_gains[b], biases[b], jnp.zeros((VEC_ROWS - 7, own), BF)]

    small = jnp.concatenate(vec_rows(0) + vec_rows(1) + [position_table], axis=0)
    packs = [pack(qkv_weight[b], out_weight[b], up_weight[b], down_weight[b]) for b in range(2)]
    small_all = lax.all_gather(small, "shard", axis=1, tiled=True).astype(F32)
    upb_all = lax.all_gather(up_bias, "shard", axis=1, tiled=True).astype(F32)
    if ringed:
        chips, cores, chunk = ring.chips, 2, own
        origin = jnp.asarray(ring.origin_table(), jnp.int32)[me]
        table = jnp.concatenate([jnp.asarray(ring.slot_table(), jnp.int32)[me], (me * segs)[None]])
        pieces = [[ring.gather(x) for x in packs[b]] for b in range(2)]
    else:
        chips, cores, chunk = 1, 1, width
        origin = jnp.zeros((1,), jnp.int32)
        table = jnp.stack([jnp.int32(0), jnp.int32(0), me * segs])
        pieces = []
        for b in range(2):
            full = [lax.all_gather(w[b], "shard", axis=0, tiled=True) for w in (qkv_weight, out_weight, up_weight, down_weight)]
            pieces.append([Pieces([(x, 0, 0)], width) for x in pack(*full)])
    place = me[None]
    vec0, vec1, tab = small_all[:VEC_ROWS], small_all[VEC_ROWS : 2 * VEC_ROWS], small_all[2 * VEC_ROWS :]

    qkv, a, o, h, hb, n1, r1 = attention_call(origin, tokens, vec0, pieces[0][0])
    y, g, gp, dz, pay, sums2 = feed_call(origin, h, cotangent, o, n1, r1, vec0, upb_all[:1], pieces[0][1], ff)

    grad_first = cotangent.reshape(segs, SEG, width)[:, 0, :]
    pay = jnp.concatenate([pay.reshape(segs, -1).astype(BF), grad_first], axis=1)
    pay_all = lax.all_gather(pay, "shard", axis=0, tiled=True)
    heads = pay_all[:, :width]
    grad_heads = pay_all[:, 4 * width + 128 :]
    cross_out, d_cross, cq, co, cu, cd, c_sums, c_up, c_tab = cross_call(
        origin, place, heads, grad_heads, docs, tab, vec1, upb_all[1:], pieces[1][0], pieces[1][1], ff, own
    )
    own_rows = lax.dynamic_slice_in_dim(cross_out, me * segs, segs, 0)
    merged = y.reshape(segs, SEG, width).at[:, 0, :].set(own_rows.astype(BF)).reshape(rows, width)

    dm, du, dz1, db, do, sums1, up_sums = feed_back_call(origin, dz, gp, n1, r1, vec0, pieces[0][1], pieces[0][0])
    main = grads_call(table, g, dm, du, hb, o, db, chips, cores, chunk)

    dz1_first, do_first, fo, fu, fd, f_sums, f_up = first_call(
        origin, place, pay_all[:, : 4 * width + 128], d_cross, vec0, upb_all[:1], pieces[0][0], pieces[0][1], ff, own
    )
    d_tokens, sums_v, *tail = attention_back_call(
        origin, table, qkv, a, do, dz1, tokens, do_first, dz1_first, pieces[0][0], chips, cores, chunk
    )

    if ringed:
        main_own = ring.reduce(*main)
        tail_own = ring.reduce(*tail)
        main_up, main_out = main_own[:, :ff], main_own[:, 2 * ff :]
        main_down = jnp.concatenate([main_own[:, ff + j * width : ff + (j + 1) * width] for j in range(group)], axis=0)
    else:
        full = main[0][0]
        down_full = jnp.concatenate([full[:, ff + j * width : ff + (j + 1) * width] for j in range(group)], axis=0)
        main_up = lax.psum_scatter(full[:, :ff], "shard", scatter_dimension=0, tiled=True)
        main_out = lax.psum_scatter(full[:, 2 * ff :], "shard", scatter_dimension=0, tiled=True)
        main_down = lax.psum_scatter(down_full, "shard", scatter_dimension=0, tiled=True)
        tail_own = lax.psum_scatter(tail[0][0], "shard", scatter_dimension=0, tiled=True)
    main_up = main_up.astype(F32) + fu.astype(F32)
    main_out = main_out.astype(F32) + fo.astype(F32)
    main_down = main_down.astype(F32) + fd.astype(F32)

    vec_sums = jnp.concatenate(
        [sums1[0:1], sums2[0:1], sums_v[0:1], sums1[2:3], sums2[2:3], sums1[1:2], sums2[1:2], jnp.zeros((1, width), F32)]
        + [up_sums[0].reshape(group, width), jnp.zeros((4, width), F32)],
        axis=0,
    )
    vec_all = sum_everywhere(vec_sums, shards)
    seg_vec = lax.dynamic_slice_in_dim(vec_all[:8], me * own, own, 1)
    seg_up = lax.dynamic_slice_in_dim(vec_all[8 : 8 + group].reshape(ff), me * own * group, own * group, 0)
    few_vec = over_seq(jnp.concatenate([f_sums, c_sums, c_tab], axis=0))
    few_up = over_seq(jnp.concatenate([f_up, c_up], axis=0))
    seg_vec = seg_vec + few_vec[:8]
    cross_vec = few_vec[8:16]
    grad_up_bias = jnp.stack([seg_up + few_up[0], few_up[8]])
    return (
        merged,
        d_tokens,
        jnp.stack([over_seq(tail_own), over_seq(cq)]),
        jnp.stack([over_seq(main_out), over_seq(co)]),
        jnp.stack([over_seq(main_up), over_seq(cu)]),
        jnp.stack([over_seq(main_down), over_seq(cd)]),
        jnp.stack([seg_vec[:2], cross_vec[:2]]),
        jnp.stack([seg_vec[2:7], cross_vec[2:7]]),
        grad_up_bias,
        few_vec[16:],
    )


def solution(mesh):
    in_specs = (
        P(("seq", "shard"), None),
        P(None, "shard", None),
        P(None, "shard", None),
        P(None, "shard", None),
        P(None, "shard", None),
        P(None, None, "shard"),
        P(None, None, "shard"),
        P(None, "shard"),
        P(None, "shard"),
        P("seq", None),
        P(("seq", "shard"), None),
    )
    out_specs = (
        P(("seq", "shard"), None),
        P(("seq", "shard"), None),
        P(None, "shard", None),
        P(None, "shard", None),
        P(None, "shard", None),
        P(None, "shard", None),
        P(None, None, "shard"),
        P(None, None, "shard"),
        P(None, "shard"),
        P(None, "shard"),
    )
    return jax.shard_map(body, mesh=mesh, in_specs=in_specs, out_specs=out_specs, check_vma=False)
```

time: 1190 us -> 535 us (0.45)
  blocking collectives: 345 us -> 69.8 us
  waiting for transfers between devices: 415 us -> 167 us
  matrix products: 188 us -> 0 us
  Pallas kernels: 0 us -> 162 us
  local copies, waits for them, and re-layouts: 157 us -> 25.3 us
  starting transfers between devices: 14.8 us -> 75.9 us
  other arithmetic: 44.3 us -> 24.7 us
  between operations: 17.4 us -> 2.32 us
    reduce_scatter x3 -> x0, waiting for transfers between devices: 207 us -> none  [the longest x1 114 us: body(): lax.psum_scatter(seg_grads[3], 'shard', scatter_dimension=0, tiled=True)]
    dot_general x38 -> x0, matrix products: 188 us -> none  [the longest x8 47.9 us: times_transposed(): lax.dot_general(left_side, right_side, (((1,), (1,)), ((), ())), preferre...]
    ppermute x0 -> x101, waiting for transfers between devices: none -> 167 us  [the longest x24 77.5 us: forward(): return lax.ppermute(x, 'shard', self.shift(1))]
    pallas_call x0 -> x7, Pallas kernels: none -> 162 us  [the longest x1 30.9 us: attention_back_call(): pl.pallas_call(partial(attention_back_kernel, pieces, chips, cores, chunk...]
    unnamed x2 -> x0, blocking collectives: 120 us -> none
    unnamed x18 -> x0, waiting for transfers between devices: 109 us -> none
    ppermute x0 -> x101, starting transfers between devices: none -> 75.9 us  [the longest x24 27.5 us: forward(): return lax.ppermute(x, 'shard', self.shift(1))]
    all_to_all x1 -> x0, blocking collectives: 74.2 us -> none  [segment_back(): lax.all_to_all(stacked, 'seq', split_axis=1, concat_axis=2, tiled=True)]
  transfers between devices with their start and end apart: 18 -> 101, of which waited for: 8 -> 36; matrix products, arithmetic and copies ran while one was open for 26% -> 8% of each run, Pallas kernels for 0% -> 22%
where the time goes in v1:
time: 535 us; the launch traced here: 527 us
  waiting for transfers between devices  167 us (31%)
  Pallas kernels  162 us (30%)
  starting transfers between devices  75.9 us (14%)
  blocking collectives  69.8 us (13%)
  local copies, waits for them, and re-layouts  25.3 us (5%)
  other arithmetic  24.7 us (5%)
    ppermute x24, waiting for transfers between devices, forward(): return lax.ppermute(x, 'shard', self.shift(1))  77.5 us
    ppermute x24, waiting for transfers between devices, backward(): return lax.ppermute(x, 'shard', self.shift(-1))  72.9 us
    pallas_call x1, Pallas kernels, attention_back_call(): pl.pallas_call(partial(attention_back_kernel, pieces, chips, cores, chunk...  30.9 us
    ppermute x24, starting transfers between devices, forward(): return lax.ppermute(x, 'shard', self.shift(1))  27.5 us
    all_gather x1, blocking collectives, body(): small_all = lax.all_gather(small, 'shard', axis=1, tiled=True).astype(F32)  27.4 us
    ppermute x24, starting transfers between devices, backward(): return lax.ppermute(x, 'shard', self.shift(-1))  25.8 us
    pallas_call x1, Pallas kernels, first_call(): pl.pallas_call(partial(first_kernel, pa, pb, width, ff, chunk), in_specs=...  24.8 us
    pallas_call x1, Pallas kernels, grads_call(): pl.pallas_call(partial(grads_kernel, chips, cores, chunk, width, ff), gri...  22.8 us
  transfers between devices with their start and end apart: 101, of which 36 were waited for; matrix products, arithmetic and copies ran while one was open for 8% of the time, Pallas kernels for 22%

profile of v1, /device:TPU:0, one launch (start us, length us, event | category | flops | bytes accessed | tf_op | source)
XLA Modules:
  0.0 527.1 jit_solution(17192276764135213980)
XLA Ops:
  8.3 5.5 %collective-permute-done.3.refs_7_.refs_28_.refs_10_.refs_13_ = bf16[48,3072]{1,0:T(8,128)(2,1)S(1)} collective-permute-done((bf16[48,3072]{1,0:T(8,128)(2,1)S(1)}, bf16[48,3072]{1,0:T(8,128)(2,1)S(1)}, u32[]{:S(2)}, u32[]{:S(2)}) %collective-permute-start.3) | collective-permute-done | bytes 294944 | tf_op jit(solution)/shard_map/ppermute | solution.py:828
  22.6 15.5 %collective-permute-done.7.refs_11_.refs_32_.refs_14_.refs_17_ = bf16[48,3072]{1,0:T(8,128)(2,1)S(1)} collective-permute-done((bf16[48,3072]{1,0:T(8,128)(2,1)S(1)}, bf16[48,3072]{1,0:T(8,128)(2,1)S(1)}, u32[]{:S(2)}, u32[]{:S(2)}) %collective-permute-start.7) | collective-permute-done | bytes 294944 | tf_op jit(solution)/shard_map/ppermute | solution.py:828
  42.2 12.4 %collective-permute-done.18.refs_10_.refs_8_.refs_26_ = bf16[48,6144]{1,0:T(8,128)(2,1)} collective-permute-done((bf16[48,6144]{1,0:T(8,128)(2,1)S(1)}, bf16[48,6144]{1,0:T(8,128)(2,1)}, u32[]{:S(2)}, u32[]{:S(2)}) %collective-permute-start.18) | collective-permute-done | bytes 589856 | tf_op jit(solution)/shard_map/ppermute | solution.py:825
  56.6 10.6 %collective-permute-done.52.refs_29_ = bf16[48,6144]{1,0:T(8,128)(2,1)} collective-permute-done((bf16[48,6144]{1,0:T(8,128)(2,1)S(1)}, bf16[48,6144]{1,0:T(8,128)(2,1)}, u32[]{:S(2)}, u32[]{:S(2)}) %collective-permute-start.52) | collective-permute-done | bytes 589856 | tf_op jit(solution)/shard_map/ppermute | solution.py:825
  90.3 11.8 %collective-permute-done.47.refs_23_ = bf16[16,3072]{1,0:T(8,128)(2,1)S(1)} collective-permute-done((bf16[16,3072]{1,0:T(8,128)(2,1)S(1)}, bf16[16,3072]{1,0:T(8,128)(2,1)S(1)}, u32[]{:S(2)}, u32[]{:S(2)}) %collective-permute-start.47) | collective-permute-done | bytes 98336 | tf_op jit(solution)/shard_map/ppermute | solution.py:825
  103.6 21.8 %all-gather = bf16[16,192,2]{1,2,0:T(2,128)(2,1)S(1)} all-gather(bf16[1,192,2]{1,2,0:T(2,128)(2,1)S(1)} %bitcast.163), channel_id=1, replica_groups=mesh['seq'=2,'shard'=16] {'shard'}, dimensions={0}, use_global_device_ids=true | all-gather | bytes 13056 | tf_op jit(solution)/shard_map/all_gather | solution.py:944
  130.8 11.7 %collective-permute-done.58.refs_35_ = bf16[48,6144]{1,0:T(8,128)(2,1)} collective-permute-done((bf16[48,6144]{1,0:T(8,128)(2,1)}, bf16[48,6144]{1,0:T(8,128)(2,1)}, u32[]{:S(2)}, u32[]{:S(2)}) %collective-permute-start.58) | collective-permute-done | bytes 589856 | tf_op jit(solution)/shard_map/ppermute | solution.py:828
  142.6 12.4 %collective-permute-done.28.refs_20_.refs_18_.refs_36_ = bf16[48,6144]{1,0:T(8,128)(2,1)S(1)} collective-permute-done((bf16[48,6144]{1,0:T(8,128)(2,1)}, bf16[48,6144]{1,0:T(8,128)(2,1)S(1)}, u32[]{:S(2)}, u32[]{:S(2)}) %collective-permute-start.28) | collective-permute-done | bytes 589856 | tf_op jit(solution)/shard_map/ppermute | solution.py:828
  155.6 27.4 %all_gather.9 = bf16[96,768]{0,1:T(8,128)(2,1)S(1)} all-gather(bf16[96,48]{0,1:T(8,128)(2,1)S(1)} %concatenate.50), channel_id=1, replica_groups=mesh['seq'=2,'shard'=16] {'shard'}, dimensions={1}, use_global_device_ids=true | all-gather | bytes 156672 | tf_op jit(solution)/shard_map/all_gather | solution.py:943
  194.9 17.5 %segment_attention.1 = (bf16[1024,2304]{1,0:T(8,128)(2,1)}, bf16[8,6,256,128]{3,2,1,0:T(8,128)(2,1)}, bf16[1024,768]{1,0:T(8,128)(2,1)}, f32[1024,768]{1,0:T(8,1...) custom-call(s32[16]{0:T(128)} %fusion.28.refs_0_, bf16[1024,768]{1,0:T(8,128)(2,1)} %refs_6_.1, ...), custom_call_target="tpu_custom_call" | custom-call | flops 6039797760 | bytes 12582912 | tf_op jit(solution)/shard_map/segment_attention/pallas_call | solution.py:179
  215.7 22.3 %segment_feed.1 = (bf16[1024,768]{1,0:T(8,128)(2,1)}, bf16[1024,3072]{1,0:T(8,128)(2,1)}, bf16[1024,3072]{1,0:T(8,128)(2,1)}, f32[1024,768]{1,0:T(8,128)}, f32[4,2,3200]{2,1,0:T(2,128)}, /*index=5*/f32[8,768]{1,0:T(8,128)}) custom-call(s32[16]{0:T(128)} %fusion.28.refs_0_, f32[1024,768]{1,0:T(8,128)} %get-tuple-element.64.refs_1_, ...), custom_call_target="tpu_custom_call" | custom-call | flops 9663676416 | bytes 12582912 | tf_op jit(solution)/shard_map/segment_feed/pallas_call | solution.py:283
  243.3 7.8 %collective-permute-done.66.refs_43_ = bf16[32,6144]{1,0:T(8,128)(2,1)S(1)} collective-permute-done((bf16[32,6144]{1,0:T(8,128)(2,1)S(1)}, bf16[32,6144]{1,0:T(8,128)(2,1)S(1)}, u32[]{:S(2)}, u32[]{:S(2)}) %collective-permute-start.66) | collective-permute-done | bytes 393248 | tf_op jit(solution)/shard_map/ppermute | solution.py:828
  251.2 20.6 %all_gather.11 = bf16[128,3968]{1,0:T(8,128)(2,1)S(1)} all-gather(bf16[8,3968]{1,0:T(8,128)(2,1)S(1)} %pad_maximum_fusion.10), channel_id=1, replica_groups=mesh['seq'=2,'shard'=16] {'shard'}, dimensions={0}, use_global_device_ids=true | all-gather | bytes 1079296 | tf_op jit(solution)/shard_map/all_gather | solution.py:966
  275.9 21.2 %cross_block.1 = (f32[128,768]{1,0:T(8,128)}, f32[128,768]{1,0:T(8,128)}, bf16[48,2304]{1,0:T(8,128)(2,1)}, bf16[48,768]{1,0:T(8,128)(2,1)}, bf16[48,3072]{1,0:T...) custom-call(s32[16]{0:T(128)} %fusion.28.refs_0_, ...), custom_call_target="tpu_custom_call" | custom-call | flops 4831838208 | bytes 11796480 | tf_op jit(solution)/shard_map/cross_block/pallas_call | solution.py:709
  297.1 24.8 %first_rows.1 = (f32[128,768]{1,0:T(8,128)}, f32[128,768]{1,0:T(8,128)}, bf16[48,768]{1,0:T(8,128)(2,1)}, bf16[48,3072]{1,0:T(8,128)(2,1)}, bf16[192,768]{1,0:T(...) custom-call(s32[16]{0:T(128)} %fusion.28.refs_0_, s32[1]{0:T(128)} %bitcast.16.refs_1_, ...), custom_call_target="tpu_custom_call" | custom-call | flops 4227858432 | bytes 8847360 | tf_op jit(solution)/shard_map/first_rows/pallas_call | solution.py:781
  324.2 22.3 %segment_feed_back.1 = (bf16[1024,768]{1,0:T(8,128)(2,1)}, bf16[1024,3072]{1,0:T(8,128)(2,1)}, f32[1024,768]{1,0:T(8,128)}, bf16[1024,768]{1,0:T(8,128)(2,1)}, b...) custom-call(s32[16]{0:T(128)} %fusion.28.refs_0_, f32[1024,768]{1,0:T(8,128)} %get-tuple-element.73.refs_1_, ...), custom_call_target="tpu_custom_call" | custom-call | flops 10871635968 | bytes 12582912 | tf_op jit(solution)/shard_map/segment_feed_back/pallas_call | solution.py:376
  347.4 30.9 %segment_attention_back.1 = (bf16[1024,768]{1,0:T(8,128)(2,1)}, f32[8,768]{1,0:T(8,128)}, bf16[8,48,2304]{2,1,0:T(8,128)(2,1)}, bf16[8,48,2304]{2,1,0:T(8,128)(2,1)}) custom-call(s32[16]{0:T(128)} %fusion.28.refs_0_, s32[10]{0:T(128)} %pad_add_fusion.refs_1_.refs_0_, bf16[1024,2304]{1,0:T(8,128)(2,1)} %get-tuple-element.71.refs_2_, ...), custom_call_target="tpu_custom_call" | custom-call | flops 9663676416 | bytes 15728640 | tf_op jit(solution)/shard_map/segment_attention_back/pallas_call | solution.py:544
  380.9 22.8 %segment_grads.1 = (bf16[8,48,6912]{2,1,0:T(8,128)(2,1)}, bf16[8,48,6912]{2,1,0:T(8,128)(2,1)}) custom-call(s32[10]{0:T(128)} %pad_add_fusion.refs_1_.refs_0_, bf16[1024,3072]{1,0:T(8,128)(2,1)} %get-tuple-element.84.refs_1_, bf16[1024,768]{1,0:T(8,128)(2,1)} %get-tuple-element.85.refs_2_, bf16[1024,3072]{1,0:T(8,128)(2,1)} %get-tuple-element.86.refs_3_, ...), custom_call_target="tpu_custom_call" | custom-call | flops 10871635968 | bytes 33816576 | tf_op jit(solution)/shard_map/segment_grads/pallas_call | solution.py:469
  440.5 4.0 collective-permute-done.69
  457.1 6.0 %collective-permute-done.80 = bf16[16,6912]{1,0:T(8,128)(2,1)S(1)} collective-permute-done((bf16[16,6912]{1,0:T(8,128)(2,1)S(1)}, bf16[16,6912]{1,0:T(8,128)(2,1)S(1)}, u32[]{:S(2)}, u32[]{:S(2)}) %collective-permute-start.80) | collective-permute-done | bytes 221216 | tf_op jit(solution)/shard_map/ppermute | solution.py:825
  470.3 9.0 %collective-permute-done.81 = bf16[48,6912]{1,0:T(8,128)(2,1)S(1)} collective-permute-done((bf16[48,6912]{1,0:T(8,128)(2,1)S(1)}, bf16[48,6912]{1,0:T(8,128)(2,1)S(1)}, u32[]{:S(2)}, u32[]{:S(2)}) %collective-permute-start.81) | collective-permute-done | bytes 663584 | tf_op jit(solution)/shard_map/ppermute | solution.py:825
  479.4 4.4 collective-permute-done.85
  490.3 6.0 %collective-permute-done.82 = bf16[48,6912]{1,0:T(8,128)(2,1)S(1)} collective-permute-done((bf16[48,6912]{1,0:T(8,128)(2,1)S(1)}, bf16[48,6912]{1,0:T(8,128)(2,1)S(1)}, u32[]{:S(2)}, u32[]{:S(2)}) %collective-permute-start.82) | collective-permute-done | bytes 663584 | tf_op jit(solution)/shard_map/ppermute | solution.py:825
  503.8 8.9 %collective-permute-done.83 = bf16[48,6912]{1,0:T(8,128)(2,1)S(1)} collective-permute-done((bf16[48,6912]{1,0:T(8,128)(2,1)S(1)}, bf16[48,6912]{1,0:T(8,128)(2,1)S(1)}, u32[]{:S(2)}, u32[]{:S(2)}) %collective-permute-start.83) | collective-permute-done | bytes 663584 | tf_op jit(solution)/shard_map/ppermute | solution.py:825
  (452 shorter events, 166.9 us)
Async XLA Ops:
  15.7 26.3 %collective-permute-start.20 = (bf16[48,6144]{1,0:T(8,128)(2,1)S(1)}, bf16[48,6144]{1,0:T(8,128)(2,1)}, u32[]{:S(2)}, u32[]{:S(2)}) collective-permute-start(bf16[48,6144]{1,0:T(8,128)(2,1)S(1)} %get-tuple-element.167.refs_8_.refs_6_.refs_24_), channel_id=1, source_target_pairs={{0,2},{1,3},{4,0},{5,1},{8,4},{9,5},{12,8},{13,9},{14,12},{15,13},... | collective-permute-start | bytes 1769480 | tf_op jit(solution)/shard_map/ppermute | solution.py:828
  40.3 26.9 %collective-permute-start.52 = (bf16[48,6144]{1,0:T(8,128)(2,1)S(1)}, bf16[48,6144]{1,0:T(8,128)(2,1)}, u32[]{:S(2)}, u32[]{:S(2)}) collective-permute-start(bf16[48,6144]{1,0:T(8,128)(2,1)S(1)} %get-tuple-element.166.refs_27_), channel_id=1, source_target_pairs={{0,4},{1,5},{4,8},{5,9},{8,12},{9,13},{12,14},{13,15},{14,10},{15,... | collective-permute-start | bytes 1769480 | tf_op jit(solution)/shard_map/ppermute | solution.py:825
  83.0 43.0 %collective-permute-start.24 = (bf16[48,6144]{1,0:T(8,128)(2,1)}, bf16[48,6144]{1,0:T(8,128)(2,1)}, u32[]{:S(2)}, u32[]{:S(2)}) collective-permute-start(bf16[48,6144]{1,0:T(8,128)(2,1)} %collective-permute-done.20.refs_12_.refs_10_.refs_28_), channel_id=1, source_target_pairs={{0,2},{1,3},{4,0},{5,1},{8,4},{9,5},{12,8},{13,9},{14,12},{15,13},... | collective-permute-start | bytes 1769480 | tf_op jit(solution)/shard_map/ppermute | solution.py:828
  86.3 41.7 %collective-permute-start.22 = (bf16[48,6144]{1,0:T(8,128)(2,1)}, bf16[48,6144]{1,0:T(8,128)(2,1)}, u32[]{:S(2)}, u32[]{:S(2)}) collective-permute-start(bf16[48,6144]{1,0:T(8,128)(2,1)} %collective-permute-done.18.refs_10_.refs_8_.refs_26_), channel_id=1, source_target_pairs={{0,4},{1,5},{4,8},{5,9},{8,12},{9,13},{12,14},{13,15},{14,10},{15,... | collective-permute-start | bytes 1769480 | tf_op jit(solution)/shard_map/ppermute | solution.py:825
  88.1 40.0 %collective-permute-start.19 = (bf16[48,6144]{1,0:T(8,128)(2,1)}, bf16[48,6144]{1,0:T(8,128)(2,1)}, u32[]{:S(2)}, u32[]{:S(2)}) collective-permute-start(bf16[48,6144]{1,0:T(8,128)(2,1)} %collective-permute-done.18.refs_10_.refs_8_.refs_26_), channel_id=1, source_target_pairs={{0,1},{1,0},{2,3},{3,2},{4,5},{5,4},{6,7},{7,6},{8,9},{9,8},{10,11... | collective-permute-start | bytes 1769480 | tf_op jit(solution)/shard_map/ppermute | solution.py:831
  125.6 57.6 %collective-permute-start.21 = (bf16[48,6144]{1,0:T(8,128)(2,1)}, bf16[48,6144]{1,0:T(8,128)(2,1)}, u32[]{:S(2)}, u32[]{:S(2)}) collective-permute-start(bf16[48,6144]{1,0:T(8,128)(2,1)} %collective-permute-done.20.refs_12_.refs_10_.refs_28_), channel_id=1, source_target_pairs={{0,1},{1,0},{2,3},{3,2},{4,5},{5,4},{6,7},{7,6},{8,9},{9,8},{10,11... | collective-permute-start | bytes 1769480 | tf_op jit(solution)/shard_map/ppermute | solution.py:831
  128.0 27.0 %collective-permute-start.28 = (bf16[48,6144]{1,0:T(8,128)(2,1)}, bf16[48,6144]{1,0:T(8,128)(2,1)S(1)}, u32[]{:S(2)}, u32[]{:S(2)}) collective-permute-start(bf16[48,6144]{1,0:T(8,128)(2,1)} %collective-permute-done.24.refs_16_.refs_14_.refs_32_), channel_id=1, source_target_pairs={{0,2},{1,3},{4,0},{5,1},{8,4},{9,5},{12,8},{13,9},{14,12},{15,13},... | collective-permute-start | bytes 1769480 | tf_op jit(solution)/shard_map/ppermute | solution.py:828
  128.1 55.4 %collective-permute-start.26 = (bf16[48,6144]{1,0:T(8,128)(2,1)}, bf16[48,6144]{1,0:T(8,128)(2,1)}, u32[]{:S(2)}, u32[]{:S(2)}) collective-permute-start(bf16[48,6144]{1,0:T(8,128)(2,1)} %collective-permute-done.22.refs_14_.refs_12_.refs_30_), channel_id=1, source_target_pairs={{0,4},{1,5},{4,8},{5,9},{8,12},{9,13},{12,14},{13,15},{14,10},{15,... | collective-permute-start | bytes 1769480 | tf_op jit(solution)/shard_map/ppermute | solution.py:825
  142.5 46.7 %collective-permute-start.23 = (bf16[48,6144]{1,0:T(8,128)(2,1)}, bf16[48,6144]{1,0:T(8,128)(2,1)}, u32[]{:S(2)}, u32[]{:S(2)}) collective-permute-start(bf16[48,6144]{1,0:T(8,128)(2,1)} %collective-permute-done.22.refs_14_.refs_12_.refs_30_), channel_id=1, source_target_pairs={{0,1},{1,0},{2,3},{3,2},{4,5},{5,4},{6,7},{7,6},{8,9},{9,8},{10,11... | collective-permute-start | bytes 1769480 | tf_op jit(solution)/shard_map/ppermute | solution.py:831
  142.5 46.6 %collective-permute-start.62 = (bf16[48,6144]{1,0:T(8,128)(2,1)}, bf16[48,6144]{1,0:T(8,128)(2,1)S(1)}, u32[]{:S(2)}, u32[]{:S(2)}) collective-permute-start(bf16[48,6144]{1,0:T(8,128)(2,1)} %collective-permute-done.58.refs_35_), channel_id=1, source_target_pairs={{0,2},{1,3},{4,0},{5,1},{8,4},{9,5},{12,8},{13,9},{14,12},{15,13},... | collective-permute-start | bytes 1769480 | tf_op jit(solution)/shard_map/ppermute | solution.py:828
  155.0 34.7 %collective-permute-start.60 = (bf16[48,6144]{1,0:T(8,128)(2,1)}, bf16[48,6144]{1,0:T(8,128)(2,1)}, u32[]{:S(2)}, u32[]{:S(2)}) collective-permute-start(bf16[48,6144]{1,0:T(8,128)(2,1)} %collective-permute-done.56.refs_33_), channel_id=1, source_target_pairs={{0,4},{1,5},{4,8},{5,9},{8,12},{9,13},{12,14},{13,15},{14,10},{15,... | collective-permute-start | bytes 1769480 | tf_op jit(solution)/shard_map/ppermute | solution.py:825
  213.4 26.2 %collective-permute-start.53 = (bf16[48,6144]{1,0:T(8,128)(2,1)}, bf16[48,6144]{1,0:T(8,128)(2,1)}, u32[]{:S(2)}, u32[]{:S(2)}) collective-permute-start(bf16[48,6144]{1,0:T(8,128)(2,1)} %collective-permute-done.52.refs_29_), channel_id=1, source_target_pairs={{0,1},{1,0},{2,3},{3,2},{4,5},{5,4},{6,7},{7,6},{8,9},{9,8},{10,11... | collective-permute-start | bytes 1769480 | tf_op jit(solution)/shard_map/ppermute | solution.py:831
  214.0 26.0 %collective-permute-start.55 = (bf16[48,6144]{1,0:T(8,128)(2,1)S(1)}, bf16[48,6144]{1,0:T(8,128)(2,1)}, u32[]{:S(2)}, u32[]{:S(2)}) collective-permute-start(bf16[48,6144]{1,0:T(8,128)(2,1)S(1)} %copy-done.35), channel_id=1, source_target_pairs={{0,1},{1,0},{2,3},{3,2},{4,5},{5,4},{6,7},{7,6},{8,9},{9,8},{10,11... | collective-permute-start | bytes 1769480 | tf_op jit(solution)/shard_map/ppermute | solution.py:831
  214.9 28.0 %collective-permute-start.57 = (bf16[48,6144]{1,0:T(8,128)(2,1)}, bf16[48,6144]{1,0:T(8,128)(2,1)}, u32[]{:S(2)}, u32[]{:S(2)}) collective-permute-start(bf16[48,6144]{1,0:T(8,128)(2,1)} %collective-permute-done.56.refs_33_), channel_id=1, source_target_pairs={{0,1},{1,0},{2,3},{3,2},{4,5},{5,4},{6,7},{7,6},{8,9},{9,8},{10,11... | collective-permute-start | bytes 1769480 | tf_op jit(solution)/shard_map/ppermute | solution.py:831
  240.8 33.2 %collective-permute-start.59 = (bf16[48,6144]{1,0:T(8,128)(2,1)}, bf16[48,6144]{1,0:T(8,128)(2,1)S(1)}, u32[]{:S(2)}, u32[]{:S(2)}) collective-permute-start(bf16[48,6144]{1,0:T(8,128)(2,1)} %collective-permute-done.58.refs_35_), channel_id=1, source_target_pairs={{0,1},{1,0},{2,3},{3,2},{4,5},{5,4},{6,7},{7,6},{8,9},{9,8},{10,11... | collective-permute-start | bytes 1769480 | tf_op jit(solution)/shard_map/ppermute | solution.py:831
  241.1 31.7 %collective-permute-start.64 = (bf16[16,6144]{1,0:T(8,128)(2,1)S(1)}, bf16[16,6144]{1,0:T(8,128)(2,1)S(1)}, u32[]{:S(2)}, u32[]{:S(2)}) collective-permute-start(bf16[16,6144]{1,0:T(8,128)(2,1)S(1)} %slice.548), channel_id=1, source_target_pairs={{0,4},{1,5},{4,8},{5,9},{8,12},{9,13},{12,14},{13,15},{14,10},{15,... | collective-permute-start | bytes 589832 | tf_op jit(solution)/shard_map/ppermute | solution.py:825
  242.8 31.4 %collective-permute-start.61 = (bf16[48,6144]{1,0:T(8,128)(2,1)}, bf16[48,6144]{1,0:T(8,128)(2,1)S(1)}, u32[]{:S(2)}, u32[]{:S(2)}) collective-permute-start(bf16[48,6144]{1,0:T(8,128)(2,1)} %collective-permute-done.60.refs_37_), channel_id=1, source_target_pairs={{0,1},{1,0},{2,3},{3,2},{4,5},{5,4},{6,7},{7,6},{8,9},{9,8},{10,11... | collective-permute-start | bytes 1769480 | tf_op jit(solution)/shard_map/ppermute | solution.py:831
  242.9 31.4 %collective-permute-start.63 = (bf16[48,6144]{1,0:T(8,128)(2,1)S(1)}, bf16[48,6144]{1,0:T(8,128)(2,1)S(1)}, u32[]{:S(2)}, u32[]{:S(2)}) collective-permute-start(bf16[48,6144]{1,0:T(8,128)(2,1)S(1)} %collective-permute-done.62.refs_39_), channel_id=1, source_target_pairs={{0,1},{1,0},{2,3},{3,2},{4,5},{5,4},{6,7},{7,6},{8,9},{9,8},{10,11... | collective-permute-start | bytes 1769480 | tf_op jit(solution)/shard_map/ppermute | solution.py:831
  322.7 85.2 %collective-permute-start.100 = (bf16[16,192]{1,0:T(8,128)(2,1)S(1)}, bf16[16,192]{1,0:T(8,128)(2,1)S(1)}, u32[]{:S(2)}, u32[]{:S(2)}) collective-permute-start(bf16[16,192]{1,0:T(8,128)(2,1)S(1)} %pad_maximum_fusion.13), channel_id=1, source_target_pairs={{0,16},{16,0},{1,17},{17,1},{2,18},{18,2},{3,19},{19,3},{4,20},{20... | collective-permute-start | bytes 18440 | tf_op jit(solution)/shard_map/ppermute | solution.py:891
  380.1 28.8 %collective-permute-start.94 = (bf16[16,768]{1,0:T(8,128)(2,1)S(1)}, bf16[16,768]{1,0:T(8,128)(2,1)S(1)}, u32[]{:S(2)}, u32[]{:S(2)}) collective-permute-start(bf16[16,768]{1,0:T(8,128)(2,1)S(1)} %concatenate.62), channel_id=1, source_target_pairs={{0,1},{1,0},{2,3},{3,2},{4,5},{5,4},{6,7},{7,6},{8,9},{9,8},{10,11... | collective-permute-start | bytes 73736 | tf_op jit(solution)/shard_map/ppermute | solution.py:903
  380.3 30.2 %collective-permute-start.99 = (bf16[80,48]{1,0:T(8,128)(2,1)S(1)}, bf16[80,48]{1,0:T(8,128)(2,1)S(1)}, u32[]{:S(2)}, u32[]{:S(2)}) collective-permute-start(bf16[80,48]{1,0:T(8,128)(2,1)S(1)} %pad_maximum_fusion.11), channel_id=1, source_target_pairs={{0,16},{16,0},{1,17},{17,1},{2,18},{18,2},{3,19},{19,3},{4,20},{20... | collective-permute-start | bytes 23048 | tf_op jit(solution)/shard_map/ppermute | solution.py:891
  403.7 49.5 %collective-permute-start.79 = (bf16[8,48,6912]{2,1,0:T(8,128)(2,1)}, bf16[8,48,6912]{2,1,0:T(8,128)(2,1)}, u32[]{:S(2)}, u32[]{:S(2)}) collective-permute-start(bf16[8,48,6912]{2,1,0:T(8,128)(2,1)} %get-tuple-element.90), channel_id=1, source_target_pairs={{0,1},{1,0},{2,3},{3,2},{4,5},{5,4},{6,7},{7,6},{8,9},{9,8},{10,11... | collective-permute-start | bytes 15925256 | tf_op jit(solution)/shard_map/ppermute | solution.py:831
  403.9 42.8 %collective-permute-start.93 = (bf16[192,768]{1,0:T(8,128)(2,1)}, bf16[192,768]{1,0:T(8,128)(2,1)}, u32[]{:S(2)}, u32[]{:S(2)}) collective-permute-start(bf16[192,768]{1,0:T(8,128)(2,1)} %get-tuple-element.96), channel_id=1, source_target_pairs={{0,16},{16,0},{1,17},{17,1},{2,18},{18,2},{3,19},{19,3},{4,20},{20... | collective-permute-start | bytes 884744 | tf_op jit(solution)/shard_map/ppermute | solution.py:891
  407.8 29.3 %collective-permute-start.91 = (bf16[48,3072]{1,0:T(8,128)(2,1)}, bf16[48,3072]{1,0:T(8,128)(2,1)}, u32[]{:S(2)}, u32[]{:S(2)}) collective-permute-start(bf16[48,3072]{1,0:T(8,128)(2,1)} %get-tuple-element.94), channel_id=1, source_target_pairs={{0,16},{16,0},{1,17},{17,1},{2,18},{18,2},{3,19},{19,3},{4,20},{20... | collective-permute-start | bytes 884744 | tf_op jit(solution)/shard_map/ppermute | solution.py:891
  (147 other events, 4020.1 us)
